TPU v7x, 256 devices: a whole 4x4x8 slice. The times are simulated.
256 devices in a mesh: row: 32 (over y, z), col: 8 (over x, core).
Axes of the slice: x: 4, y: 4, z: 8, core: 2. Of those that a mesh axis runs over, the one named last changes fastest.
Arguments:
- acts: bfloat16 [6144, 28672], P('col', 'row'), may hold values from -12 to 12
- out_grad: bfloat16 [6144, 8192], P('row', 'col'), may hold values from -12 to 12
- lengths: int32 [8], replicated, may hold values from 1 to 768, 4800 in all
Outputs:
- weight_grad: bfloat16 [28672, 8192], P('row', 'col')
- norms: float32 [8], replicated
All inputs are finite; a program needn't handle non-finite values.
Results may differ from a plain program's by a relative error of at most 0.0013.
Values may be sent and summed in bfloat16 or wider, within the bound.
No kernel may reach another device: no remote copies, remote signals or barrier semaphores. Data moves between devices by JAX's collectives and lax.ppermute only.
A program may use at most 128 MiB of HBM per device.

v0:
```python
import jax
import jax.numpy as jnp
from jax import lax
from jax.sharding import PartitionSpec as P

FF = 28672
D = 8192


def body(acts, out_grad, lengths):
    n_row = lax.axis_size("row")
    n_col = lax.axis_size("col")
    row_idx = lax.axis_index("row")
    col_idx = lax.axis_index("col")
    own_rows = out_grad.shape[0]
    tokens = own_rows * n_row
    seqs = lengths.shape[0]
    seq_len = tokens // seqs
    block = own_rows // n_col
    feats = acts.shape[1]
    width = out_grad.shape[1]
    positions = jnp.arange(tokens, dtype=jnp.int32)
    seq_of = positions // seq_len
    limit = jnp.sum(
        jnp.where(
            seq_of[:, None] == jnp.arange(seqs, dtype=jnp.int32)[None, :], lengths[None, :], 0
        ),
        axis=1,
    )
    live = positions % seq_len < limit
    act_full = lax.all_gather(acts, "col", axis=0, tiled=True)
    grad_full = lax.all_gather(out_grad, "row", axis=0, tiled=True)
    grads = jnp.where(live[:, None], grad_full, jnp.zeros_like(grad_full))
    act_seq = act_full.reshape(seqs, seq_len, feats)
    picked = lax.dynamic_index_in_dim(
        act_full.reshape(n_row, n_col, block, feats), col_idx, 1, keepdims=False
    )
    picked = picked.reshape(seqs, n_row // seqs * block, feats)
    act_part = jnp.einsum("sqf,slf->sql", picked, act_seq, preferred_element_type=jnp.float32)
    act_part = act_part.reshape(n_row * block, seq_len)
    summed = lax.psum(act_part.astype(jnp.bfloat16), "row").astype(jnp.float32)
    act_gram = lax.dynamic_slice_in_dim(summed, row_idx * block, block, 0)
    first = row_idx * own_rows
    own_seq = first // seq_len
    own_grads = lax.dynamic_slice_in_dim(grads, first, own_rows, 0)
    seq_grads = lax.dynamic_slice_in_dim(grads, own_seq * seq_len, seq_len, 0)
    grad_part = lax.dot_general(
        own_grads, seq_grads, (((1,), (1,)), ((), ())), preferred_element_type=jnp.float32
    )
    grad_gram = lax.psum_scatter(
        grad_part.astype(jnp.bfloat16), "col", scatter_dimension=0, tiled=True
    ).astype(jnp.float32)
    local = jnp.sum(act_gram * grad_gram)
    onehot = jnp.arange(seqs, dtype=jnp.int32) == own_seq
    squares = lax.psum(jnp.where(onehot, local, jnp.float32(0.0)), ("row", "col"))
    divisor = float(FF) * float(D) * float(seq_len)
    norms = jnp.sqrt(squares / divisor)
    scale = 1.0 / (norms + 0.1)
    total = jnp.zeros((feats, width), jnp.float32)
    for seq in range(seqs):
        act_rows = act_full[seq * seq_len : (seq + 1) * seq_len]
        grad_rows = grads[seq * seq_len : (seq + 1) * seq_len]
        product = lax.dot_general(
            act_rows, grad_rows, (((0,), (0,)), ((), ())), preferred_element_type=jnp.float32
        )
        total = total + scale[seq] * product
    weight_grad = (total / jnp.sqrt(jnp.float32(tokens))).astype(jnp.bfloat16)
    return (weight_grad, norms)


def solution(mesh):
    placed = (P("col", "row"), P("row", "col"), P())
    return jax.shard_map(
        body, mesh=mesh, in_specs=placed, out_specs=(P("row", "col"), P()), check_vma=False
    )
```

profile of v0, /device:TPU:1, one launch (start us, length us, event | category | flops | bytes accessed | tf_op | source)
XLA Modules:
  0.0 494.6 jit_solution(12963730170209471229)
XLA Ops:
  7.2 0.7 all-gather.3.cloned.1.call-update
  7.9 0.7 all-gather.5.cloned.1.call-update
  8.7 0.8 select_reduce_fusion
  9.6 67.8 %all-gather.3.cloned.1.call-done = bf16[6144,896]{1,0:T(8,128)(2,1)} async-done(((bf16[768,896]{1,0:T(8,128)(2,1)}), bf16[6144,896]{1,0:T(8,128)(2,1)}) %all-gather.3.cloned.1.call-update) | async-done | bytes 11010064 | tf_op jit(solution)/shard_map/all_gather | solution.py:31
  77.3 1.5 constant_dynamic-slice_fusion
  78.8 8.6 %convolution_convert_fusion = bf16[8,96,768]{2,1,0:T(8,128)(2,1)} fusion(bf16[8,96,896]{2,1,0:T(8,128)(2,1)S(1)} %bitcast.20, bf16[8,768,896]{2,1,0:T(8,128)(2,1)} %bitcast.19), kind=kOutput, calls=%fused_computation.20 | convolution fusion | flops 1057554432 | bytes 13565952 | tf_op jit(solution)/shard_map/sqf,slf->sql/dot_general | solution.py:39
  87.7 111.5 %all-gather.5.cloned.1.call-done = bf16[6144,1024]{1,0:T(8,128)(2,1)} async-done(((bf16[192,1024]{1,0:T(8,128)(2,1)}), bf16[6144,1024]{1,0:T(8,128)(2,1)}) %all-gather.5.cloned.1.call-update) | async-done | bytes 12582928 | tf_op jit(solution)/shard_map/all_gather | solution.py:32
  199.2 6.4 %broadcast_select_fusion = bf16[6144,1024]{1,0:T(8,128)(2,1)S(1)} fusion(bf16[6144,1024]{1,0:T(8,128)(2,1)} %all-gather.5.cloned.1.call-done, pred[6144]{0:T(1024)(128)(4,1)S(1)} %fusion.32), kind=kLoop, calls=%fused_computation | loop fusion | flops 6291456 | bytes 25171968 | tf_op jit(solution)/shard_map/jit(_where)/select_n | solution.py:33
  205.6 4.5 copy-done
  210.1 1.4 fusion.28
  211.6 5.7 %fusion.1 = f32[1024,896]{1,0:T(8,128)} fusion(bf16[6144,1024]{1,0:T(8,128)(2,1)} %copy-done, bf16[6144,896]{1,0:T(8,128)(2,1)} %all-gather.3.cloned.1.call-done), kind=kOutput, calls=%fused_computation.3 | convolution fusion | flops 1409286144 | bytes 6619136 | tf_op jit(solution)/shard_map/dot_general | solution.py:63
  217.3 5.7 %fusion.3 = f32[1024,896]{1,0:T(8,128)} fusion(bf16[6144,1024]{1,0:T(8,128)(2,1)} %copy-done, bf16[6144,896]{1,0:T(8,128)(2,1)} %all-gather.3.cloned.1.call-done), kind=kOutput, calls=%fused_computation.5 | convolution fusion | flops 1409286144 | bytes 6619136 | tf_op jit(solution)/shard_map/dot_general | solution.py:63
  223.0 5.0 %fusion.5 = f32[1024,896]{1,0:T(8,128)} fusion(bf16[6144,1024]{1,0:T(8,128)(2,1)S(1)} %copy-done.1, bf16[6144,896]{1,0:T(8,128)(2,1)} %all-gather.3.cloned.1.call-done), kind=kOutput, calls=%fused_computation.7 | convolution fusion | flops 1409286144 | bytes 6619136 | tf_op jit(solution)/shard_map/dot_general | solution.py:63
  228.0 5.1 %fusion.7 = f32[1024,896]{1,0:T(8,128)} fusion(bf16[6144,1024]{1,0:T(8,128)(2,1)S(1)} %copy-done.1, bf16[6144,896]{1,0:T(8,128)(2,1)} %all-gather.3.cloned.1.call-done), kind=kOutput, calls=%fused_computation.9 | convolution fusion | flops 1409286144 | bytes 6619136 | tf_op jit(solution)/shard_map/dot_general | solution.py:63
  233.1 5.0 %fusion.9 = f32[1024,896]{1,0:T(8,128)} fusion(bf16[6144,1024]{1,0:T(8,128)(2,1)S(1)} %copy-done.1, bf16[6144,896]{1,0:T(8,128)(2,1)} %all-gather.3.cloned.1.call-done), kind=kOutput, calls=%fused_computation.11 | convolution fusion | flops 1409286144 | bytes 6619136 | tf_op jit(solution)/shard_map/dot_general | solution.py:63
  238.1 5.0 %fusion.11 = f32[1024,896]{1,0:T(8,128)} fusion(bf16[6144,1024]{1,0:T(8,128)(2,1)S(1)} %copy-done.1, bf16[6144,896]{1,0:T(8,128)(2,1)} %all-gather.3.cloned.1.call-done), kind=kOutput, calls=%fused_computation.13 | convolution fusion | flops 1409286144 | bytes 6619136 | tf_op jit(solution)/shard_map/dot_general | solution.py:63
  243.1 102.7 %all-reduce.2.cloned.1.call-done = bf16[768,768]{1,0:T(8,128)(2,1)} async-done(((bf16[768,768]{1,0:T(8,128)(2,1)}), bf16[768,768]{1,0:T(8,128)(2,1)}) %all-reduce.2.cloned.1.call-update) | async-done | bytes 1179664 | tf_op jit(solution)/shard_map/psum | solution.py:41
  345.8 35.1 %reduce-scatter.2.cloned.1.call-done = bf16[24,768]{1,0:T(8,128)(2,1)} async-done(((bf16[192,768]{1,0:T(8,128)(2,1)}), bf16[24,768]{1,0:T(8,128)(2,1)}) %reduce-scatter.2.cloned.1.call-update) | async-done | bytes 36880 | tf_op jit(solution)/shard_map/reduce_scatter | solution.py:50
  380.9 1.4 multiply_reduce_fusion
  382.3 0.6 compare_select_fusion
  383.0 5.5 %fusion.13 = f32[1024,896]{1,0:T(8,128)} fusion(bf16[6144,1024]{1,0:T(8,128)(2,1)} %copy-done, bf16[6144,896]{1,0:T(8,128)(2,1)} %all-gather.3.cloned.1.call-done), kind=kOutput, calls=%fused_computation.15 | convolution fusion | flops 1409286144 | bytes 6619136 | tf_op jit(solution)/shard_map/dot_general | solution.py:63
  388.4 78.6 %psum.15 = f32[8]{0:T(128)S(1)} all-reduce(f32[8]{0:T(128)S(1)} %compare_select_fusion), channel_id=1, replica_groups=mesh['row'=32,'col'=8] {'row','col'}, use_global_device_ids=true, to_apply=%region_4.5 | all-reduce | flops 8 | bytes 64 | tf_op jit(solution)/shard_map/psum | solution.py:55
  468.2 17.5 %fusion.17 = bf16[896,1024]{0,1:T(8,128)(2,1)S(1)} fusion(bf16[6144,1024]{1,0:T(8,128)(2,1)} %copy-done, f32[]{:T(128)} %bitcast.11, f32[1024,896]{1,0:T(8,128)} %fusion.1, f32[]{:T(128)} %bitcast.10, f32[1024,896]{1,0:T(8,128)} %fusion.3, f32[]{:T(128)} %bitcast.9, f32[1024,896]{1,0:T(8,128)} %fusion.5, f32[]{:T(128)} %bitcast.8, f32[1024,896]{1,0:T(8,128)} %fusion.7, ...), kind=kOutput, calls=%fused_computation.19 | convolution fusion | flops 1424883712 | bytes 30478336 | tf_op jit(solution)/shard_map/dot_general | solution.py:63
  485.7 2.4 copy.8
  (13 shorter events, 1.6 us)
Async XLA Ops:
  7.2 70.2 %all-gather.3.cloned.1.call-start = ((), (), s32[]{:S(2)}) async-start(), calls=%async_computation.1 | async-start | bytes 12386304 | tf_op jit(solution)/shard_map/all_gather | solution.py:31
  7.9 191.3 %all-gather.5.cloned.1.call-start = ((), (), s32[]{:S(2)}) async-start(), calls=%async_computation.3 | async-start | bytes 12976128 | tf_op jit(solution)/shard_map/all_gather | solution.py:32
  8.6 337.2 %all-reduce.2.cloned.1.call-start = ((), (), s32[]{:S(2)}) async-start(), calls=%async_computation.2 | async-start | bytes 2359296 | tf_op jit(solution)/shard_map/psum | solution.py:41
  87.5 293.4 %reduce-scatter.2.cloned.1.call-start = ((), (), s32[]{:S(2)}) async-start(), calls=%async_computation.4 | async-start | bytes 331776 | tf_op jit(solution)/shard_map/reduce_scatter | solution.py:50
  205.6 4.6 copy-start
  211.6 11.4 %copy-start.1 = (bf16[6144,1024]{1,0:T(8,128)(2,1)S(1)}, bf16[6144,1024]{1,0:T(8,128)(2,1)}, u32[]{:S(2)}) copy-start(bf16[6144,1024]{1,0:T(8,128)(2,1)} %copy-done) | copy-start | bytes 37748740
Sparse Core Ops, SparseCore 0:
  9.8 67.4 all-gather.2
  79.9 119.2 all-gather.4
  203.2 142.5 all-reduce.1
  348.2 32.6 reduce-scatter.1
where the time goes:
time: 495 us
  waiting for transfers between devices  318 us (64%)
  blocking collectives  78.6 us (16%)
  matrix products  64.5 us (13%)
  between operations  13.9 us (3%)
  other arithmetic  9.76 us (2%)
  local copies, waits for them, and re-layouts  9.06 us (2%)
    all_gather x1, waiting for transfers between devices, body(): grad_full = lax.all_gather(out_grad, 'row', axis=0, tiled=True)  112 us
    psum x1, waiting for transfers between devices, body(): summed = lax.psum(act_part.astype(jnp.bfloat16), 'row').astype(jnp.float32)  103 us
    psum x1, blocking collectives, body(): lax.psum(jnp.where(onehot, local, jnp.float32(0.0)), ('row', 'col'))  78.6 us
    all_gather x1, waiting for transfers between devices, body(): act_full = lax.all_gather(acts, 'col', axis=0, tiled=True)  67.8 us
    dot_general x8, matrix products, body(): lax.dot_general(act_rows, grad_rows, (((0,), (0,)), ((), ())), preferred_...  54.5 us
    reduce_scatter x1, waiting for transfers between devices, body(): lax.psum_scatter(grad_part.astype(jnp.bfloat16), 'col', scatter_dimension...  35.1 us
  transfers between devices with their start and end apart: 4, of which 4 were waited for; matrix products, arithmetic and copies ran while one was open for 10% of the time, Pallas kernels for 0%

commit v1 on v0

v1 whole, which is shorter than its diff:
```python
import jax
import jax.numpy as jnp
from jax import lax
from jax.sharding import PartitionSpec as P

FF = 28672
D = 8192


def body(acts, out_grad, lengths):
    n_row = lax.axis_size("row")
    own_rows = out_grad.shape[0]
    tokens = own_rows * n_row
    seqs = lengths.shape[0]
    seq_len = tokens // seqs
    slot = lax.broadcasted_iota(jnp.int32, (seq_len, 1), 0)
    act_full = lax.all_gather(acts, "col", axis=0, tiled=True)
    grad_full = lax.all_gather(out_grad, "row", axis=0, tiled=True)
    products = []
    locals_ = []
    for seq in range(seqs):
        act_rows = act_full[seq * seq_len : (seq + 1) * seq_len]
        grad_rows = grad_full[seq * seq_len : (seq + 1) * seq_len]
        grad_rows = jnp.where(slot < lengths[seq], grad_rows, jnp.zeros_like(grad_rows))
        product = lax.dot_general(
            act_rows, grad_rows, (((0,), (0,)), ((), ())), preferred_element_type=jnp.float32
        )
        products.append(product)
        locals_.append(jnp.sum(product * product))
    squares = lax.psum(jnp.stack(locals_), ("row", "col"))
    divisor = float(FF) * float(D) * float(seq_len)
    norms = jnp.sqrt(squares / divisor)
    scale = 1.0 / (norms + 0.1)
    total = scale[0] * products[0]
    for seq in range(1, seqs):
        total = total + scale[seq] * products[seq]
    weight_grad = (total / jnp.sqrt(jnp.float32(tokens))).astype(jnp.bfloat16)
    return (weight_grad, norms)


def solution(mesh):
    placed = (P("col", "row"), P("row", "col"), P())
    return jax.shard_map(
        body, mesh=mesh, in_specs=placed, out_specs=(P("row", "col"), P()), check_vma=False
    )
```

time: 495 us -> 345 us (0.70)
  waiting for transfers between devices: 318 us -> 185 us
  matrix products: 64.5 us -> 39.3 us
  other arithmetic: 9.76 us -> 20.9 us
    psum x1 -> x0, waiting for transfers between devices: 103 us -> none  [body(): summed = lax.psum(act_part.astype(jnp.bfloat16), 'row').astype(jnp.float32)]
    reduce_scatter x1 -> x0, waiting for transfers between devices: 35.1 us -> none  [body(): lax.psum_scatter(grad_part.astype(jnp.bfloat16), 'col', scatter_dimension...]
    convert_element_type x0 -> x1, other arithmetic: none -> 15.4 us  [body(): weight_grad = (total / jnp.sqrt(jnp.float32(tokens))).astype(jnp.bfloat16)]
    dot_general x8, matrix products: 54.5 us -> 39.3 us  [body(): lax.dot_general(act_rows, grad_rows, (((0,), (0,)), ((), ())), preferred_...]
    all_gather x1, waiting for transfers between devices: 112 us -> 122 us  [body(): grad_full = lax.all_gather(out_grad, 'row', axis=0, tiled=True)]
    dot_general x2 -> x0, matrix products: 10.1 us -> none  [the longest x1 8.65 us: body(): jnp.einsum('sqf,slf->sql', picked, act_seq, preferred_element_type=jnp.fl...]
    select_n x3 -> x0, other arithmetic: 7.03 us -> none  [the longest x1 6.37 us: body(): grads = jnp.where(live[:, None], grad_full, jnp.zeros_like(grad_full))]
    all_gather x1, waiting for transfers between devices: 67.8 us -> 62 us  [body(): act_full = lax.all_gather(acts, 'col', axis=0, tiled=True)]
  transfers between devices with their start and end apart: 4 -> 2, of which waited for: 4 -> 2; matrix products, arithmetic and copies ran while one was open for 10% -> 2% of each run, Pallas kernels for 0% -> 0%
where the time goes in v1:
time: 345 us
  waiting for transfers between devices  185 us (54%)
  blocking collectives  74.9 us (22%)
  matrix products  39.3 us (11%)
  other arithmetic  20.9 us (6%)
  between operations  14.1 us (4%)
  local copies, waits for them, and re-layouts  10.2 us (3%)
    all_gather x1, waiting for transfers between devices, body(): grad_full = lax.all_gather(out_grad, 'row', axis=0, tiled=True)  122 us
    psum x1, blocking collectives, body(): squares = lax.psum(jnp.stack(locals_), ('row', 'col'))  74.9 us
    all_gather x1, waiting for transfers between devices, body(): act_full = lax.all_gather(acts, 'col', axis=0, tiled=True)  62 us
    dot_general x8, matrix products, body(): lax.dot_general(act_rows, grad_rows, (((0,), (0,)), ((), ())), preferred_...  39.3 us
    convert_element_type x1, other arithmetic, body(): weight_grad = (total / jnp.sqrt(jnp.float32(tokens))).astype(jnp.bfloat16)  15.4 us
  transfers between devices with their start and end apart: 2, of which 2 were waited for; matrix products, arithmetic and copies ran while one was open for 2% of the time, Pallas kernels for 0%

profile of v1, /device:TPU:1, one launch (start us, length us, event | category | flops | bytes accessed | tf_op | source)
XLA Modules:
  0.0 344.8 jit_solution(8986895510977710011)
XLA Ops:
  7.2 0.7 all-gather.5.cloned.1.call-update
  7.9 0.7 all-gather.3.cloned.1.call-update
  8.6 1.6 fusion.42
  10.3 0.7 iota_compare_fusion.1
  10.9 0.7 iota_compare_fusion.2
  12.2 0.7 iota_compare_fusion.4
  12.9 0.6 iota_compare_fusion.5
  13.5 0.6 iota_compare_fusion.6
  14.1 0.6 iota_compare_fusion.7
  15.3 62.0 %all-gather.5.cloned.1.call-done = bf16[6144,896]{1,0:T(8,128)(2,1)} async-done(((bf16[768,896]{1,0:T(8,128)(2,1)}), bf16[6144,896]{1,0:T(8,128)(2,1)}) %all-gather.5.cloned.1.call-update) | async-done | bytes 11010064 | tf_op jit(solution)/shard_map/all_gather | solution.py:17
  77.3 121.9 %all-gather.3.cloned.1.call-done = bf16[6144,1024]{1,0:T(8,128)(2,1)} async-done(((bf16[192,1024]{1,0:T(8,128)(2,1)}), bf16[6144,1024]{1,0:T(8,128)(2,1)}) %all-gather.3.cloned.1.call-update) | async-done | bytes 12582928 | tf_op jit(solution)/shard_map/all_gather | solution.py:18
  199.2 6.4 %multiply_reduce_fusion = (f32[]{:T(128)}, f32[1024,896]{1,0:T(8,128)}) fusion(bf16[6144,896]{1,0:T(8,128)(2,1)} %all-gather.5.cloned.1.call-done, bf16[6144,1024]{1,0:T(8,128)(2,1)} %all-gather.3.cloned.1.call-done, pred[768]{0:T(1024)(128)(4,1)S(1)} %iota_compare_fusion), kind=kOutput, calls=%fused_computation.1 | convolution fusion | flops 1411907584 | bytes 6619908 | tf_op jit(solution)/shard_map/dot_general | solution.py:25
  206.0 5.9 %multiply_reduce_fusion.7 = (f32[]{:T(128)}, f32[1024,896]{1,0:T(8,128)}) fusion(bf16[6144,896]{1,0:T(8,128)(2,1)} %all-gather.5.cloned.1.call-done, bf16[6144,1024]{1,0:T(8,128)(2,1)S(1)} %copy-done, pred[768]{0:T(1024)(128)(4,1)S(1)} %iota_compare_fusion.7), kind=kOutput, calls=%fused_computation.8 | convolution fusion | flops 1411907584 | bytes 6620164 | tf_op jit(solution)/shard_map/dot_general | solution.py:25
  211.8 4.5 %multiply_reduce_fusion.6 = (f32[]{:T(128)}, f32[1024,896]{1,0:T(8,128)}) fusion(bf16[6144,896]{1,0:T(8,128)(2,1)S(1)} %copy-done.1, bf16[6144,1024]{1,0:T(8,128)(2,1)S(1)} %copy-done, pred[768]{0:T(1024)(128)(4,1)S(1)} %iota_compare_fusion.6), kind=kOutput, calls=%fused_computation.7 | convolution fusion | flops 1411907584 | bytes 6620164 | tf_op jit(solution)/shard_map/dot_general | solution.py:25
  216.3 4.5 %multiply_reduce_fusion.5 = (f32[]{:T(128)}, f32[1024,896]{1,0:T(8,128)}) fusion(bf16[6144,896]{1,0:T(8,128)(2,1)S(1)} %copy-done.1, bf16[6144,1024]{1,0:T(8,128)(2,1)S(1)} %copy-done, pred[768]{0:T(1024)(128)(4,1)S(1)} %iota_compare_fusion.5), kind=kOutput, calls=%fused_computation.6 | convolution fusion | flops 1411907584 | bytes 6620164 | tf_op jit(solution)/shard_map/dot_general | solution.py:25
  220.8 4.5 %multiply_reduce_fusion.4 = (f32[]{:T(128)}, f32[1024,896]{1,0:T(8,128)}) fusion(bf16[6144,896]{1,0:T(8,128)(2,1)S(1)} %copy-done.1, bf16[6144,1024]{1,0:T(8,128)(2,1)S(1)} %copy-done, pred[768]{0:T(1024)(128)(4,1)S(1)} %iota_compare_fusion.4), kind=kOutput, calls=%fused_computation.5 | convolution fusion | flops 1411907584 | bytes 6620164 | tf_op jit(solution)/shard_map/dot_general | solution.py:25
  225.3 4.4 %multiply_reduce_fusion.3 = (f32[]{:T(128)}, f32[1024,896]{1,0:T(8,128)}) fusion(bf16[6144,896]{1,0:T(8,128)(2,1)S(1)} %copy-done.1, bf16[6144,1024]{1,0:T(8,128)(2,1)S(1)} %copy-done, pred[768]{0:T(1024)(128)(4,1)S(1)} %iota_compare_fusion.3), kind=kOutput, calls=%fused_computation.4 | convolution fusion | flops 1411907584 | bytes 6620164 | tf_op jit(solution)/shard_map/dot_general | solution.py:25
  229.8 4.6 %multiply_reduce_fusion.2 = (f32[]{:T(128)}, f32[1024,896]{1,0:T(8,128)}) fusion(bf16[6144,896]{1,0:T(8,128)(2,1)S(1)} %copy-done.1, bf16[6144,1024]{1,0:T(8,128)(2,1)S(1)} %copy-done, pred[768]{0:T(1024)(128)(4,1)S(1)} %iota_compare_fusion.2), kind=kOutput, calls=%fused_computation.3 | convolution fusion | flops 1411907584 | bytes 6620164 | tf_op jit(solution)/shard_map/dot_general | solution.py:25
  234.4 4.5 %multiply_reduce_fusion.1 = (f32[]{:T(128)}, f32[1024,896]{1,0:T(8,128)}) fusion(bf16[6144,896]{1,0:T(8,128)(2,1)S(1)} %copy-done.1, bf16[6144,1024]{1,0:T(8,128)(2,1)S(1)} %copy-done, pred[768]{0:T(1024)(128)(4,1)S(1)} %iota_compare_fusion.1), kind=kOutput, calls=%fused_computation.2 | convolution fusion | flops 1411907584 | bytes 6620164 | tf_op jit(solution)/shard_map/dot_general | solution.py:25
  238.9 5.1 %stack.35 = f32[8]{0:T(128)S(1)} concatenate(f32[1]{0:T(128)} %bitcast.1, f32[1]{0:T(128)} %bitcast.3, f32[1]{0:T(128)} %bitcast.5, f32[1]{0:T(128)} %bitcast.7, f32[1]{0:T(128)} %bitcast.9, f32[1]{0:T(128)} %bitcast.11, f32[1]{0:T(128)} %bitcast.13, f32[1]{0:T(128)} %bitcast.15), dimensions={0} | concatenate | bytes 64 | tf_op jit(solution)/shard_map/stack | solution.py:30
  244.0 74.9 %psum.7 = f32[8]{0:T(128)S(1)} all-reduce(f32[8]{0:T(128)S(1)} %stack.35), channel_id=1, replica_groups=mesh['row'=32,'col'=8] {'row','col'}, use_global_device_ids=true, to_apply=%region_8.9 | all-reduce | flops 8 | bytes 64 | tf_op jit(solution)/shard_map/psum | solution.py:30
  319.5 0.7 fusion.41
  320.1 15.4 %fusion = bf16[896,1024]{0,1:T(8,128)(2,1)S(1)} fusion(f32[1024,896]{1,0:T(8,128)} %get-tuple-element.37, f32[]{:T(128)} %bitcast.23, f32[1024,896]{1,0:T(8,128)} %get-tuple-element.35, f32[]{:T(128)} %bitcast.22, f32[1024,896]{1,0:T(8,128)} %get-tuple-element.33, f32[]{:T(128)} %bitcast.21, f32[1024,896]{1,0:T(8,128)} %get-tuple-element.31, f32[]{:T(128)} %bitcast.20, ...), kind=kLoop, calls=%fused_computation.9 | loop fusion | flops 15597568 | bytes 31195168 | tf_op jit(solution)/shard_map/convert_element_type | solution.py:37
  335.6 2.4 copy.5
  (9 shorter events, 2.2 us)
Async XLA Ops:
  7.2 70.2 %all-gather.5.cloned.1.call-start = ((), (), s32[]{:S(2)}) async-start(), calls=%async_computation.1 | async-start | bytes 12386304 | tf_op jit(solution)/shard_map/all_gather | solution.py:17
  7.9 191.3 %all-gather.3.cloned.1.call-start = ((), (), s32[]{:S(2)}) async-start(), calls=%async_computation | async-start | bytes 12976128 | tf_op jit(solution)/shard_map/all_gather | solution.py:18
  199.2 6.8 %copy-start = (bf16[6144,1024]{1,0:T(8,128)(2,1)S(1)}, bf16[6144,1024]{1,0:T(8,128)(2,1)}, u32[]{:S(2)}) copy-start(bf16[6144,1024]{1,0:T(8,128)(2,1)} %all-gather.3.cloned.1.call-done) | copy-start | bytes 37748740
  206.0 5.9 %copy-start.1 = (bf16[6144,896]{1,0:T(8,128)(2,1)S(1)}, bf16[6144,896]{1,0:T(8,128)(2,1)}, u32[]{:S(2)}) copy-start(bf16[6144,896]{1,0:T(8,128)(2,1)} %all-gather.5.cloned.1.call-done) | copy-start | bytes 33030148
Sparse Core Ops, SparseCore 0:
  9.8 67.4 all-gather.4
  79.9 119.2 all-gather.2

commit v2 on v1

v2 whole, which is shorter than its diff:
```python
import math

import jax
import jax.numpy as jnp
from jax import lax
from jax.experimental import pallas as pl
from jax.experimental.pallas import tpu as pltpu
from jax.sharding import PartitionSpec as P

FF = 28672
D = 8192
SEQS = 8
LEN = 768
NY = 4
NZ = 8
OWN = SEQS * LEN // (NY * NZ)
ORDER = (0, 1, 3, 2)


def z_shift(value, step):
    pairs = [(i, i // NZ * NZ + (i % NZ + step) % NZ) for i in range(NY * NZ)]
    return lax.ppermute(value, "row", pairs)


def y_shift(value, step):
    pairs = [(i, (i + NZ * step) % (NY * NZ)) for i in range(NY * NZ)]
    return lax.ppermute(value, "row", pairs)


def z_ring(own):
    half = own.shape[0] // 2
    up1, down1 = z_shift(own, 1), z_shift(own, -1)
    up2, down2 = z_shift(up1, 1), z_shift(down1, -1)
    up3, down3 = z_shift(up2, 1), z_shift(down2, -1)
    up4, down4 = z_shift(up3[:half], 1), z_shift(down3[half:], -1)
    return [own, down1, down2, down3, up4, down4, up3, up2, up1]


def y_ring(own):
    half = own.shape[0] // 2
    up1, down1 = y_shift(own, 1), y_shift(own, -1)
    up2, down2 = y_shift(up1[:half], 1), y_shift(down1[half:], -1)
    return [own, down1, up2, down2, up1]


def products_kernel(*refs):
    acts, left, right = refs[0], refs[1:6], refs[6:15]
    prod, squares, grads, act_buf, grad_sem, act_sem = refs[15:]
    row = lax.axis_index("row")
    y, z = row // NZ, row % NZ
    width = left[0].shape[1]

    def left_source(rel, k):
        if rel == 2:
            return left[2 + k // 4].at[pl.ds(k % 4 * OWN, OWN)]
        return left[{0: 0, 1: 1, 3: 4}[rel]].at[pl.ds(k * OWN, OWN)]

    def right_source(rel, k):
        if k == 4:
            return right[4 + rel // 2].at[pl.ds(rel % 2 * OWN, OWN)]
        return right[k if k < 4 else k + 1].at[pl.ds(rel * OWN, OWN)]

    def seq_of(i):
        pair = i // 2
        rel = jnp.where(pair == 2, 3, jnp.where(pair == 3, 2, pair))
        return 2 * ((y + rel) % NY) + i % 2

    def act_copy(i):
        start = pl.multiple_of(seq_of(i) * LEN, LEN)
        return pltpu.make_async_copy(acts.at[pl.ds(start, LEN)], act_buf.at[i % 2], act_sem.at[i % 2])

    act_copy(0).start()
    for place, rel in enumerate(ORDER):
        for k in range(NZ):
            owner = (z + k) % NZ
            slot = 2 * place + owner // 4
            rows = pl.ds(pl.multiple_of(owner % 4 * OWN, OWN), OWN)
            sem = grad_sem.at[place]
            pltpu.make_async_copy(left_source(rel, k), grads.at[slot, rows, pl.ds(0, width)], sem).start()
            pltpu.make_async_copy(right_source(rel, k), grads.at[slot, rows, pl.ds(width, width)], sem).start()

    lane = lax.broadcasted_iota(jnp.int32, squares.shape, 1)

    def step(i, acc):
        @pl.when(i + 1 < SEQS)
        def _():
            act_copy(i + 1).start()

        @pl.when(i % 2 == 0)
        def _():
            both = grads.at[pl.ds(pl.multiple_of(i, 2), 2)]
            pltpu.make_async_copy(both, both, grad_sem.at[i // 2]).wait()

        act_copy(i).wait()
        p = lax.dot_general(
            act_buf[i % 2], grads[i], (((0,), (0,)), ((), ())), preferred_element_type=jnp.float32
        )
        prod[i] = p
        return jnp.where(lane == seq_of(i), jnp.sum(p * p), acc)

    squares[...] = lax.fori_loop(0, SEQS, step, jnp.zeros(squares.shape, jnp.float32))


def combine_kernel(parts, prod, out, norms, out_buf, sem):
    row = lax.axis_index("row")
    y = row // NZ
    squares = jnp.sum(parts[...], axis=0, keepdims=True)
    norm = jnp.sqrt(squares / (float(FF) * float(D) * float(LEN)))
    norms[...] = norm
    scale = (1.0 / (norm + 0.1)) / math.sqrt(SEQS * LEN)
    lane = lax.broadcasted_iota(jnp.int32, scale.shape, 1)
    factors = []
    for i in range(SEQS):
        seq = 2 * ((y + ORDER[i // 2]) % NY) + i % 2
        factors.append(jnp.sum(jnp.where(lane == seq, scale, 0.0)))
    rows = 128
    chunks = out.shape[0] // rows

    def copy(c):
        at = pl.ds(pl.multiple_of(c * rows, rows), rows)
        return pltpu.make_async_copy(out_buf.at[at], out.at[at], sem.at[c])

    def step(c, carry):
        at = pl.ds(pl.multiple_of(c * rows, rows), rows)
        total = factors[0] * prod[0, at]
        for i in range(1, SEQS):
            total = total + factors[i] * prod[i, at]
        out_buf[at] = total.astype(jnp.bfloat16)
        copy(c).start()
        return carry

    lax.fori_loop(0, chunks, step, 0)
    for c in range(chunks):
        copy(c).wait()


def body(acts, out_grad, lengths):
    row = lax.axis_index("row")
    feats, width = acts.shape[1], out_grad.shape[1]
    devices = lax.axis_size("row") * lax.axis_size("col")
    act_full = lax.all_gather(acts, "col", axis=0, tiled=True)

    first = row * OWN
    slot = first % LEN + lax.broadcasted_iota(jnp.int32, (OWN, 1), 0)
    own = jnp.where(slot < lengths[first // LEN], out_grad, jnp.zeros_like(out_grad))
    left = z_ring(own[:, : width // 2])
    right = y_ring(own[:, width // 2 :])
    left = y_ring(jnp.concatenate(left, axis=0))
    right = z_ring(jnp.concatenate(right, axis=0))

    anywhere = pl.BlockSpec(memory_space=pl.ANY)
    vmem = pl.BlockSpec(memory_space=pltpu.VMEM)
    prod, squares = pl.pallas_call(
        products_kernel,
        out_shape=(
            pltpu.VMEM((SEQS, feats, width), jnp.float32),
            jax.ShapeDtypeStruct((devices, SEQS), jnp.float32),
        ),
        in_specs=[anywhere] * 15,
        out_specs=(vmem, vmem),
        scratch_shapes=[
            pltpu.VMEM((SEQS, LEN, width), jnp.bfloat16),
            pltpu.VMEM((2, LEN, feats), jnp.bfloat16),
            pltpu.SemaphoreType.DMA((NY,)),
            pltpu.SemaphoreType.DMA((2,)),
        ],
        compiler_params=pltpu.CompilerParams(vmem_limit_bytes=26 << 20),
        name="sequence_products",
    )(act_full, *left, *right)
    parts = lax.all_to_all(squares, ("row", "col"), 0, 0, tiled=True)
    weight_grad, norms = pl.pallas_call(
        combine_kernel,
        out_shape=(
            jax.ShapeDtypeStruct((feats, width), jnp.bfloat16),
            jax.ShapeDtypeStruct((1, SEQS), jnp.float32),
        ),
        in_specs=[vmem, vmem],
        out_specs=(anywhere, vmem),
        scratch_shapes=[
            pltpu.VMEM((feats, width), jnp.bfloat16),
            pltpu.SemaphoreType.DMA((feats // 128,)),
        ],
        compiler_params=pltpu.CompilerParams(vmem_limit_bytes=16 << 20),
        name="scaled_sum",
    )(parts, prod)
    return (weight_grad, norms.reshape(SEQS))


def solution(mesh):
    placed = (P("col", "row"), P("row", "col"), P())
    return jax.shard_map(
        body, mesh=mesh, in_specs=placed, out_specs=(P("row", "col"), P()), check_vma=False
    )
```

time: 345 us -> 190 us (0.55)
  waiting for transfers between devices: 185 us -> 58.7 us
  blocking collectives: 74.9 us -> 28 us
  matrix products: 39.3 us -> 0 us
  starting transfers between devices: 0.08 us -> 36.4 us
  Pallas kernels: 0 us -> 29 us
  other arithmetic: 20.9 us -> 0.75 us
  local copies, waits for them, and re-layouts: 10.2 us -> 22.5 us
    all_gather x1 -> x0, waiting for transfers between devices: 122 us -> none  [body(): grad_full = lax.all_gather(out_grad, 'row', axis=0, tiled=True)]
    psum x1 -> x0, blocking collectives: 74.9 us -> none  [body(): squares = lax.psum(jnp.stack(locals_), ('row', 'col'))]
    all_gather x1, waiting for transfers between devices: 62 us -> 0.01 us  [body(): act_full = lax.all_gather(acts, 'col', axis=0, tiled=True)]
    ppermute x0 -> x24, waiting for transfers between devices: none -> 58 us  [the longest x16 40.8 us: z_shift(): return lax.ppermute(value, 'row', pairs)]
    dot_general x8 -> x0, matrix products: 39.3 us -> none  [body(): lax.dot_general(act_rows, grad_rows, (((0,), (0,)), ((), ())), preferred_...]
    ppermute x0 -> x24, starting transfers between devices: none -> 36.4 us  [the longest x16 25.2 us: z_shift(): return lax.ppermute(value, 'row', pairs)]
    pallas_call x0 -> x2, Pallas kernels: none -> 29 us  [the longest x1 25.6 us: body(): pl.pallas_call(products_kernel, out_shape=(pltpu.VMEM((SEQS, feats, width...]
    all_to_all x0 -> x1, blocking collectives: none -> 28 us  [body(): parts = lax.all_to_all(squares, ('row', 'col'), 0, 0, tiled=True)]
  transfers between devices with their start and end apart: 2 -> 25, of which waited for: 2 -> 8; matrix products, arithmetic and copies ran while one was open for 2% -> 1% of each run, Pallas kernels for 0% -> 0%
where the time goes in v2:
time: 190 us
  waiting for transfers between devices  58.7 us (31%)
  starting transfers between devices  36.4 us (19%)
  Pallas kernels  29 us (15%)
  blocking collectives  28 us (15%)
  local copies, waits for them, and re-layouts  22.5 us (12%)
  between operations  14.5 us (8%)
    ppermute x16, waiting for transfers between devices, z_shift(): return lax.ppermute(value, 'row', pairs)  40.8 us
    all_to_all x1, blocking collectives, body(): parts = lax.all_to_all(squares, ('row', 'col'), 0, 0, tiled=True)  28 us
    pallas_call x1, Pallas kernels, body(): pl.pallas_call(products_kernel, out_shape=(pltpu.VMEM((SEQS, feats, width...  25.6 us
    ppermute x16, starting transfers between devices, z_shift(): return lax.ppermute(value, 'row', pairs)  25.2 us
    unnamed x42, local copies, waits for them, and re-layouts  21 us
    ppermute x8, waiting for transfers between devices, y_shift(): return lax.ppermute(value, 'row', pairs)  17.3 us
    ppermute x8, starting transfers between devices, y_shift(): return lax.ppermute(value, 'row', pairs)  11.2 us
  transfers between devices with their start and end apart: 25, of which 8 were waited for; matrix products, arithmetic and copies ran while one was open for 1% of the time, Pallas kernels for 0%

profile of v2, /device:TPU:1, one launch (start us, length us, event | category | flops | bytes accessed | tf_op | source)
XLA Modules:
  0.0 189.8 jit_solution(11522587119209414315)
XLA Ops:
  10.0 2.2 %collective-permute-start.13 = (bf16[192,512]{1,0:T(8,128)(2,1)S(1)}, bf16[192,512]{1,0:T(8,128)(2,1)S(1)}, u32[]{:S(2)}, u32[]{:S(2)}) collective-permute-start(bf16[192,512]{1,0:T(8,128)(2,1)S(1)} %get-tuple-element.10), channel_id=1, source_target_pairs={{0,64},{8,72},{16,80},{24,88},{32,96},{40,104},{48,112},{56,120},{... | collective-permute-start | bytes 589832 | tf_op jit(solution)/shard_map/ppermute | solution.py:27
  13.8 1.6 collective-permute-start.3
  15.4 3.9 %collective-permute-start = (bf16[192,512]{1,0:T(8,128)(2,1)S(1)}, bf16[192,512]{1,0:T(8,128)(2,1)S(1)}, u32[]{:S(2)}, u32[]{:S(2)}) collective-permute-start(bf16[192,512]{1,0:T(8,128)(2,1)S(1)} %get-tuple-element.13), channel_id=1, source_target_pairs={{0,56},{8,0},{16,8},{24,16},{32,24},{40,32},{48,40},{56,48},{64,12... | collective-permute-start | bytes 589832 | tf_op jit(solution)/shard_map/ppermute | solution.py:22
  19.5 2.7 %collective-permute-start.15 = (bf16[96,512]{1,0:T(8,128)(2,1)S(1)}, bf16[96,512]{1,0:T(8,128)(2,1)S(1)}, u32[]{:S(2)}, u32[]{:S(2)}) collective-permute-start(bf16[96,512]{1,0:T(8,128)(2,1)S(1)} %slice.47), channel_id=1, source_target_pairs={{0,192},{8,200},{16,208},{24,216},{32,224},{40,232},{48,240},{56,2... | collective-permute-start | bytes 294920 | tf_op jit(solution)/shard_map/ppermute | solution.py:27
  23.5 3.1 %collective-permute-start.1 = (bf16[192,512]{1,0:T(8,128)(2,1)S(1)}, bf16[192,512]{1,0:T(8,128)(2,1)S(1)}, u32[]{:S(2)}, u32[]{:S(2)}) collective-permute-start(bf16[192,512]{1,0:T(8,128)(2,1)S(1)} %collective-permute-done), channel_id=1, source_target_pairs={{0,56},{8,0},{16,8},{24,16},{32,24},{40,32},{48,40},{56,48},{64,12... | collective-permute-start | bytes 589832 | tf_op jit(solution)/shard_map/ppermute | solution.py:22
  26.7 2.9 %collective-permute-done.4 = bf16[192,512]{1,0:T(8,128)(2,1)S(1)} collective-permute-done((bf16[192,512]{1,0:T(8,128)(2,1)S(1)}, bf16[192,512]{1,0:T(8,128)(2,1)S(1)}, u32[]{:S(2)}, u32[]{:S(2)}) %collective-permute-start.4) | collective-permute-done | bytes 196640 | tf_op jit(solution)/shard_map/ppermute | solution.py:22
  29.5 2.8 %collective-permute-start.2 = (bf16[192,512]{1,0:T(8,128)(2,1)S(1)}, bf16[192,512]{1,0:T(8,128)(2,1)S(1)}, u32[]{:S(2)}, u32[]{:S(2)}) collective-permute-start(bf16[192,512]{1,0:T(8,128)(2,1)S(1)} %collective-permute-done.1), channel_id=1, source_target_pairs={{0,56},{8,0},{16,8},{24,16},{32,24},{40,32},{48,40},{56,48},{64,12... | collective-permute-start | bytes 589832 | tf_op jit(solution)/shard_map/ppermute | solution.py:22
  32.4 2.7 %collective-permute-start.16 = (bf16[768,512]{1,0:T(8,128)(2,1)S(1)}, bf16[768,512]{1,0:T(8,128)(2,1)S(1)}, u32[]{:S(2)}, u32[]{:S(2)}) collective-permute-start(bf16[768,512]{1,0:T(8,128)(2,1)S(1)} %constant_dynamic-update-slice_fusion.9.refs_6_), channel_id=1, source_target_pairs={{0,56},{8,0},{16,8},{24,16},{32,24},{40,32},{48,40},{56,48},{64,12... | collective-permute-start | bytes 2359304 | tf_op jit(solution)/shard_map/ppermute | solution.py:22
  35.8 2.8 %collective-permute-start.7 = (bf16[96,512]{1,0:T(8,128)(2,1)S(1)}, bf16[96,512]{1,0:T(8,128)(2,1)S(1)}, u32[]{:S(2)}, u32[]{:S(2)}) collective-permute-start(bf16[96,512]{1,0:T(8,128)(2,1)S(1)} %slice.42), channel_id=1, source_target_pairs={{0,56},{8,0},{16,8},{24,16},{32,24},{40,32},{48,40},{56,48},{64,12... | collective-permute-start | bytes 294920 | tf_op jit(solution)/shard_map/ppermute | solution.py:22
  38.6 16.4 %collective-permute-done.6 = bf16[96,512]{1,0:T(8,128)(2,1)S(1)} collective-permute-done((bf16[96,512]{1,0:T(8,128)(2,1)S(1)}, bf16[96,512]{1,0:T(8,128)(2,1)S(1)}, u32[]{:S(2)}, u32[]{:S(2)}) %collective-permute-start.6) | collective-permute-done | bytes 98336 | tf_op jit(solution)/shard_map/ppermute | solution.py:22
  55.2 2.7 %collective-permute-start.8 = (bf16[1536,512]{1,0:T(8,128)(2,1)S(1)}, bf16[1536,512]{1,0:T(8,128)(2,1)S(1)}, u32[]{:S(2)}, u32[]{:S(2)}) collective-permute-start(bf16[1536,512]{1,0:T(8,128)(2,1)S(1)} %constant_dynamic-update-slice_fusion.refs_1_), channel_id=1, source_target_pairs={{0,192},{8,200},{16,208},{24,216},{32,224},{40,232},{48,240},{56,2... | collective-permute-start | bytes 4718600 | tf_op jit(solution)/shard_map/ppermute | solution.py:27
  57.9 2.7 %collective-permute-start.17 = (bf16[768,512]{1,0:T(8,128)(2,1)S(1)}, bf16[768,512]{1,0:T(8,128)(2,1)S(1)}, u32[]{:S(2)}, u32[]{:S(2)}) collective-permute-start(bf16[768,512]{1,0:T(8,128)(2,1)S(1)} %collective-permute-done.16.refs_7_), channel_id=1, source_target_pairs={{0,56},{8,0},{16,8},{24,16},{32,24},{40,32},{48,40},{56,48},{64,12... | collective-permute-start | bytes 2359304 | tf_op jit(solution)/shard_map/ppermute | solution.py:22
  60.5 14.3 %collective-permute-done.20.refs_13_ = bf16[768,512]{1,0:T(8,128)(2,1)S(1)} collective-permute-done((bf16[768,512]{1,0:T(8,128)(2,1)S(1)}, bf16[768,512]{1,0:T(8,128)(2,1)S(1)}, u32[]{:S(2)}, u32[]{:S(2)}) %collective-permute-start.20) | collective-permute-done | bytes 786464 | tf_op jit(solution)/shard_map/ppermute | solution.py:22
  74.8 2.7 %collective-permute-start.18 = (bf16[768,512]{1,0:T(8,128)(2,1)S(1)}, bf16[768,512]{1,0:T(8,128)(2,1)S(1)}, u32[]{:S(2)}, u32[]{:S(2)}) collective-permute-start(bf16[768,512]{1,0:T(8,128)(2,1)S(1)} %collective-permute-done.17.refs_8_), channel_id=1, source_target_pairs={{0,56},{8,0},{16,8},{24,16},{32,24},{40,32},{48,40},{56,48},{64,12... | collective-permute-start | bytes 2359304 | tf_op jit(solution)/shard_map/ppermute | solution.py:22
  77.6 11.9 %collective-permute-done.9.refs_5_ = bf16[1536,512]{1,0:T(8,128)(2,1)S(1)} collective-permute-done((bf16[1536,512]{1,0:T(8,128)(2,1)S(1)}, bf16[1536,512]{1,0:T(8,128)(2,1)S(1)}, u32[]{:S(2)}, u32[]{:S(2)}) %collective-permute-start.9) | collective-permute-done | bytes 1572896 | tf_op jit(solution)/shard_map/ppermute | solution.py:27
  90.6 1.8 collective-permute-start.11
  92.6 2.7 %collective-permute-start.23 = (bf16[384,512]{1,0:T(8,128)(2,1)S(1)}, bf16[384,512]{1,0:T(8,128)(2,1)S(1)}, u32[]{:S(2)}, u32[]{:S(2)}) collective-permute-start(bf16[384,512]{1,0:T(8,128)(2,1)S(1)} %slice.49), channel_id=1, source_target_pairs={{0,56},{8,0},{16,8},{24,16},{32,24},{40,32},{48,40},{56,48},{64,12... | collective-permute-start | bytes 1179656 | tf_op jit(solution)/shard_map/ppermute | solution.py:22
  95.3 5.3 %collective-permute-done.22.refs_10_ = bf16[384,512]{1,0:T(8,128)(2,1)S(1)} collective-permute-done((bf16[384,512]{1,0:T(8,128)(2,1)S(1)}, bf16[384,512]{1,0:T(8,128)(2,1)S(1)}, u32[]{:S(2)}, u32[]{:S(2)}) %collective-permute-start.22) | collective-permute-done | bytes 393248 | tf_op jit(solution)/shard_map/ppermute | solution.py:22
  100.7 5.4 %collective-permute-done.10.refs_3_ = bf16[768,512]{1,0:T(8,128)(2,1)S(1)} collective-permute-done((bf16[768,512]{1,0:T(8,128)(2,1)S(1)}, bf16[768,512]{1,0:T(8,128)(2,1)S(1)}, u32[]{:S(2)}, u32[]{:S(2)}) %collective-permute-start.10) | collective-permute-done | bytes 786464 | tf_op jit(solution)/shard_map/ppermute | solution.py:27
  107.0 25.6 %sequence_products.1 = (f32[8,896,1024]{2,1,0:T(8,128)S(1)}, f32[256,8]{1,0:T(8,128)}) custom-call(bf16[6144,896]{1,0:T(8,128)(2,1)} %all-gather.2.cloned.1.call-done.refs_0_, bf16[1536,512]{1,0:T(8,128)(2,1)} %copy-done.4, bf16[1536,512]{1,0:T(8,128)(2,1)} %copy-done.3, bf16[768,512]{1,0:T(8,128)(2,1)} %copy-done.12, ...), custom_call_target="tpu_custom_call" | custom-call | tf_op jit(solution)/shard_map/sequence_products/pallas_call | solution.py:153
  132.6 9.7 %copy-done = f32[8,896,1024]{2,1,0:T(8,128)} copy-done((f32[8,896,1024]{2,1,0:T(8,128)}, f32[8,896,1024]{2,1,0:T(8,128)S(1)}, u32[]{:S(2)}) %copy-start) | copy-done | bytes 29360152
  142.3 28.0 %all_to_all.11 = f32[256,1,8]{2,1,0:T(1,128)S(1)} all-to-all(f32[256,1,8]{2,1,0:T(1,128)} %bitcast.7), channel_id=1, replica_groups=mesh['row'=32,'col'=8] {'row','col'}, dimensions={0} | all-to-all | bytes 16384 | tf_op jit(solution)/shard_map/all_to_all | solution.py:170
  170.3 9.3 %copy-done.1 = f32[8,896,1024]{2,1,0:T(8,128)S(1)} copy-done((f32[8,896,1024]{2,1,0:T(8,128)S(1)}, f32[8,896,1024]{2,1,0:T(8,128)}, u32[]{:S(2)}) %copy-start.1) | copy-done | bytes 29360152
  179.6 3.3 %scaled_sum.1 = (bf16[896,1024]{1,0:T(8,128)(2,1)}, f32[1,8]{1,0:T(1,128)}) custom-call(f32[256,8]{1,0:T(8,128)S(1)} %bitcast.6, f32[8,896,1024]{2,1,0:T(8,128)S(1)} %copy-done.1), custom_call_target="tpu_custom_call" | custom-call | tf_op jit(solution)/shard_map/scaled_sum/pallas_call | solution.py:171
  (86 shorter events, 8.9 us)
Async XLA Ops:
  7.2 99.8 %all-gather.2.cloned.1.call-start = ((), (), s32[]{:S(2)}) async-start(), calls=%async_computation.1 | async-start | bytes 12386304 | tf_op jit(solution)/shard_map/all_gather | solution.py:141
  10.0 9.3 %collective-permute-start.13 = (bf16[192,512]{1,0:T(8,128)(2,1)S(1)}, bf16[192,512]{1,0:T(8,128)(2,1)S(1)}, u32[]{:S(2)}, u32[]{:S(2)}) collective-permute-start(bf16[192,512]{1,0:T(8,128)(2,1)S(1)} %get-tuple-element.10), channel_id=1, source_target_pairs={{0,64},{8,72},{16,80},{24,88},{32,96},{40,104},{48,112},{56,120},{... | collective-permute-start | bytes 589832 | tf_op jit(solution)/shard_map/ppermute | solution.py:27
  12.2 7.2 %collective-permute-start.12 = (bf16[192,512]{1,0:T(8,128)(2,1)S(1)}, bf16[192,512]{1,0:T(8,128)(2,1)S(1)}, u32[]{:S(2)}, u32[]{:S(2)}) collective-permute-start(bf16[192,512]{1,0:T(8,128)(2,1)S(1)} %get-tuple-element.10), channel_id=1, source_target_pairs={{0,192},{8,200},{16,208},{24,216},{32,224},{40,232},{48,240},{56,2... | collective-permute-start | bytes 589832 | tf_op jit(solution)/shard_map/ppermute | solution.py:27
  13.8 9.7 %collective-permute-start.3 = (bf16[192,512]{1,0:T(8,128)(2,1)S(1)}, bf16[192,512]{1,0:T(8,128)(2,1)S(1)}, u32[]{:S(2)}, u32[]{:S(2)}) collective-permute-start(bf16[192,512]{1,0:T(8,128)(2,1)S(1)} %get-tuple-element.13), channel_id=1, source_target_pairs={{0,8},{8,16},{16,24},{24,32},{32,40},{40,48},{48,56},{56,0},{64,72... | collective-permute-start | bytes 589832 | tf_op jit(solution)/shard_map/ppermute | solution.py:22
  15.4 8.1 %collective-permute-start = (bf16[192,512]{1,0:T(8,128)(2,1)S(1)}, bf16[192,512]{1,0:T(8,128)(2,1)S(1)}, u32[]{:S(2)}, u32[]{:S(2)}) collective-permute-start(bf16[192,512]{1,0:T(8,128)(2,1)S(1)} %get-tuple-element.13), channel_id=1, source_target_pairs={{0,56},{8,0},{16,8},{24,16},{32,24},{40,32},{48,40},{56,48},{64,12... | collective-permute-start | bytes 589832 | tf_op jit(solution)/shard_map/ppermute | solution.py:22
  19.3 7.3 %collective-permute-start.14 = (bf16[96,512]{1,0:T(8,128)(2,1)S(1)}, bf16[96,512]{1,0:T(8,128)(2,1)S(1)}, u32[]{:S(2)}, u32[]{:S(2)}) collective-permute-start(bf16[96,512]{1,0:T(8,128)(2,1)S(1)} %slice.46), channel_id=1, source_target_pairs={{0,64},{8,72},{16,80},{24,88},{32,96},{40,104},{48,112},{56,120},{... | collective-permute-start | bytes 294920 | tf_op jit(solution)/shard_map/ppermute | solution.py:27
  19.5 7.2 %collective-permute-start.15 = (bf16[96,512]{1,0:T(8,128)(2,1)S(1)}, bf16[96,512]{1,0:T(8,128)(2,1)S(1)}, u32[]{:S(2)}, u32[]{:S(2)}) collective-permute-start(bf16[96,512]{1,0:T(8,128)(2,1)S(1)} %slice.47), channel_id=1, source_target_pairs={{0,192},{8,200},{16,208},{24,216},{32,224},{40,232},{48,240},{56,2... | collective-permute-start | bytes 294920 | tf_op jit(solution)/shard_map/ppermute | solution.py:27
  23.5 6.1 %collective-permute-start.4 = (bf16[192,512]{1,0:T(8,128)(2,1)S(1)}, bf16[192,512]{1,0:T(8,128)(2,1)S(1)}, u32[]{:S(2)}, u32[]{:S(2)}) collective-permute-start(bf16[192,512]{1,0:T(8,128)(2,1)S(1)} %collective-permute-done.3), channel_id=1, source_target_pairs={{0,8},{8,16},{16,24},{24,32},{32,40},{40,48},{48,56},{56,0},{64,72... | collective-permute-start | bytes 589832 | tf_op jit(solution)/shard_map/ppermute | solution.py:22
  29.5 6.1 %collective-permute-start.5 = (bf16[192,512]{1,0:T(8,128)(2,1)S(1)}, bf16[192,512]{1,0:T(8,128)(2,1)S(1)}, u32[]{:S(2)}, u32[]{:S(2)}) collective-permute-start(bf16[192,512]{1,0:T(8,128)(2,1)S(1)} %collective-permute-done.4), channel_id=1, source_target_pairs={{0,8},{8,16},{16,24},{24,32},{32,40},{40,48},{48,56},{56,0},{64,72... | collective-permute-start | bytes 589832 | tf_op jit(solution)/shard_map/ppermute | solution.py:22
  29.5 6.2 %collective-permute-start.2 = (bf16[192,512]{1,0:T(8,128)(2,1)S(1)}, bf16[192,512]{1,0:T(8,128)(2,1)S(1)}, u32[]{:S(2)}, u32[]{:S(2)}) collective-permute-start(bf16[192,512]{1,0:T(8,128)(2,1)S(1)} %collective-permute-done.1), channel_id=1, source_target_pairs={{0,56},{8,0},{16,8},{24,16},{32,24},{40,32},{48,40},{56,48},{64,12... | collective-permute-start | bytes 589832 | tf_op jit(solution)/shard_map/ppermute | solution.py:22
  32.3 25.5 %collective-permute-start.19 = (bf16[768,512]{1,0:T(8,128)(2,1)S(1)}, bf16[768,512]{1,0:T(8,128)(2,1)S(1)}, u32[]{:S(2)}, u32[]{:S(2)}) collective-permute-start(bf16[768,512]{1,0:T(8,128)(2,1)S(1)} %constant_dynamic-update-slice_fusion.9.refs_6_), channel_id=1, source_target_pairs={{0,8},{8,16},{16,24},{24,32},{32,40},{40,48},{48,56},{56,0},{64,72... | collective-permute-start | bytes 2359304 | tf_op jit(solution)/shard_map/ppermute | solution.py:22
  32.4 25.4 %collective-permute-start.16 = (bf16[768,512]{1,0:T(8,128)(2,1)S(1)}, bf16[768,512]{1,0:T(8,128)(2,1)S(1)}, u32[]{:S(2)}, u32[]{:S(2)}) collective-permute-start(bf16[768,512]{1,0:T(8,128)(2,1)S(1)} %constant_dynamic-update-slice_fusion.9.refs_6_), channel_id=1, source_target_pairs={{0,56},{8,0},{16,8},{24,16},{32,24},{40,32},{48,40},{56,48},{64,12... | collective-permute-start | bytes 2359304 | tf_op jit(solution)/shard_map/ppermute | solution.py:22
  35.7 19.3 %collective-permute-start.6 = (bf16[96,512]{1,0:T(8,128)(2,1)S(1)}, bf16[96,512]{1,0:T(8,128)(2,1)S(1)}, u32[]{:S(2)}, u32[]{:S(2)}) collective-permute-start(bf16[96,512]{1,0:T(8,128)(2,1)S(1)} %slice.41), channel_id=1, source_target_pairs={{0,8},{8,16},{16,24},{24,32},{32,40},{40,48},{48,56},{56,0},{64,72... | collective-permute-start | bytes 294920 | tf_op jit(solution)/shard_map/ppermute | solution.py:22
  35.8 19.2 %collective-permute-start.7 = (bf16[96,512]{1,0:T(8,128)(2,1)S(1)}, bf16[96,512]{1,0:T(8,128)(2,1)S(1)}, u32[]{:S(2)}, u32[]{:S(2)}) collective-permute-start(bf16[96,512]{1,0:T(8,128)(2,1)S(1)} %slice.42), channel_id=1, source_target_pairs={{0,56},{8,0},{16,8},{24,16},{32,24},{40,32},{48,40},{56,48},{64,12... | collective-permute-start | bytes 294920 | tf_op jit(solution)/shard_map/ppermute | solution.py:22
  55.1 34.3 %collective-permute-start.9 = (bf16[1536,512]{1,0:T(8,128)(2,1)S(1)}, bf16[1536,512]{1,0:T(8,128)(2,1)S(1)}, u32[]{:S(2)}, u32[]{:S(2)}) collective-permute-start(bf16[1536,512]{1,0:T(8,128)(2,1)S(1)} %constant_dynamic-update-slice_fusion.refs_1_), channel_id=1, source_target_pairs={{0,64},{8,72},{16,80},{24,88},{32,96},{40,104},{48,112},{56,120},{... | collective-permute-start | bytes 4718600 | tf_op jit(solution)/shard_map/ppermute | solution.py:27
  55.2 34.4 %collective-permute-start.8 = (bf16[1536,512]{1,0:T(8,128)(2,1)S(1)}, bf16[1536,512]{1,0:T(8,128)(2,1)S(1)}, u32[]{:S(2)}, u32[]{:S(2)}) collective-permute-start(bf16[1536,512]{1,0:T(8,128)(2,1)S(1)} %constant_dynamic-update-slice_fusion.refs_1_), channel_id=1, source_target_pairs={{0,192},{8,200},{16,208},{24,216},{32,224},{40,232},{48,240},{56,2... | collective-permute-start | bytes 4718600 | tf_op jit(solution)/shard_map/ppermute | solution.py:27
  57.8 17.0 %collective-permute-start.20 = (bf16[768,512]{1,0:T(8,128)(2,1)S(1)}, bf16[768,512]{1,0:T(8,128)(2,1)S(1)}, u32[]{:S(2)}, u32[]{:S(2)}) collective-permute-start(bf16[768,512]{1,0:T(8,128)(2,1)S(1)} %collective-permute-done.19.refs_14_), channel_id=1, source_target_pairs={{0,8},{8,16},{16,24},{24,32},{32,40},{40,48},{48,56},{56,0},{64,72... | collective-permute-start | bytes 2359304 | tf_op jit(solution)/shard_map/ppermute | solution.py:22
  57.9 16.9 %collective-permute-start.17 = (bf16[768,512]{1,0:T(8,128)(2,1)S(1)}, bf16[768,512]{1,0:T(8,128)(2,1)S(1)}, u32[]{:S(2)}, u32[]{:S(2)}) collective-permute-start(bf16[768,512]{1,0:T(8,128)(2,1)S(1)} %collective-permute-done.16.refs_7_), channel_id=1, source_target_pairs={{0,56},{8,0},{16,8},{24,16},{32,24},{40,32},{48,40},{56,48},{64,12... | collective-permute-start | bytes 2359304 | tf_op jit(solution)/shard_map/ppermute | solution.py:22
  74.8 17.6 %collective-permute-start.21 = (bf16[768,512]{1,0:T(8,128)(2,1)S(1)}, bf16[768,512]{1,0:T(8,128)(2,1)S(1)}, u32[]{:S(2)}, u32[]{:S(2)}) collective-permute-start(bf16[768,512]{1,0:T(8,128)(2,1)S(1)} %collective-permute-done.20.refs_13_), channel_id=1, source_target_pairs={{0,8},{8,16},{16,24},{24,32},{32,40},{40,48},{48,56},{56,0},{64,72... | collective-permute-start | bytes 2359304 | tf_op jit(solution)/shard_map/ppermute | solution.py:22
  74.8 17.7 %collective-permute-start.18 = (bf16[768,512]{1,0:T(8,128)(2,1)S(1)}, bf16[768,512]{1,0:T(8,128)(2,1)S(1)}, u32[]{:S(2)}, u32[]{:S(2)}) collective-permute-start(bf16[768,512]{1,0:T(8,128)(2,1)S(1)} %collective-permute-done.17.refs_8_), channel_id=1, source_target_pairs={{0,56},{8,0},{16,8},{24,16},{32,24},{40,32},{48,40},{56,48},{64,12... | collective-permute-start | bytes 2359304 | tf_op jit(solution)/shard_map/ppermute | solution.py:22
  89.5 16.6 %collective-permute-start.10 = (bf16[768,512]{1,0:T(8,128)(2,1)S(1)}, bf16[768,512]{1,0:T(8,128)(2,1)S(1)}, u32[]{:S(2)}, u32[]{:S(2)}) collective-permute-start(bf16[768,512]{1,0:T(8,128)(2,1)S(1)} %slice.43), channel_id=1, source_target_pairs={{0,64},{8,72},{16,80},{24,88},{32,96},{40,104},{48,112},{56,120},{... | collective-permute-start | bytes 2359304 | tf_op jit(solution)/shard_map/ppermute | solution.py:27
  90.6 16.4 %collective-permute-start.11 = (bf16[768,512]{1,0:T(8,128)(2,1)S(1)}, bf16[768,512]{1,0:T(8,128)(2,1)}, u32[]{:S(2)}, u32[]{:S(2)}) collective-permute-start(bf16[768,512]{1,0:T(8,128)(2,1)S(1)} %slice.44), channel_id=1, source_target_pairs={{0,192},{8,200},{16,208},{24,216},{32,224},{40,232},{48,240},{56,2... | collective-permute-start | bytes 2359304 | tf_op jit(solution)/shard_map/ppermute | solution.py:27
  92.4 8.2 %collective-permute-start.22 = (bf16[384,512]{1,0:T(8,128)(2,1)S(1)}, bf16[384,512]{1,0:T(8,128)(2,1)S(1)}, u32[]{:S(2)}, u32[]{:S(2)}) collective-permute-start(bf16[384,512]{1,0:T(8,128)(2,1)S(1)} %slice.48), channel_id=1, source_target_pairs={{0,8},{8,16},{16,24},{24,32},{32,40},{40,48},{48,56},{56,0},{64,72... | collective-permute-start | bytes 1179656 | tf_op jit(solution)/shard_map/ppermute | solution.py:22
  92.6 8.1 %collective-permute-start.23 = (bf16[384,512]{1,0:T(8,128)(2,1)S(1)}, bf16[384,512]{1,0:T(8,128)(2,1)S(1)}, u32[]{:S(2)}, u32[]{:S(2)}) collective-permute-start(bf16[384,512]{1,0:T(8,128)(2,1)S(1)} %slice.49), channel_id=1, source_target_pairs={{0,56},{8,0},{16,8},{24,16},{32,24},{40,32},{48,40},{56,48},{64,12... | collective-permute-start | bytes 1179656 | tf_op jit(solution)/shard_map/ppermute | solution.py:22
  (17 other events, 246.5 us)
Sparse Core Ops, SparseCore 0:
  9.8 67.4 all-gather.1

commit v3 on v2

--- a/solution.py
+++ b/solution.py
@@ -1,3 +1,4 @@
+import functools
 import math
 
 import jax
@@ -14,6 +15,7 @@
 NY = 4
 NZ = 8
 OWN = SEQS * LEN // (NY * NZ)
+SENT = 3
 ORDER = (0, 1, 3, 2)
 
 
@@ -45,7 +47,7 @@
 
 def products_kernel(*refs):
     acts, left, right = refs[0], refs[1:6], refs[6:15]
-    prod, squares, grads, act_buf, grad_sem, act_sem = refs[15:]
+    kept, sent, squares, grads, act_buf, stage, grad_sem, act_sem, sent_sem = refs[15:]
     row = lax.axis_index("row")
     y, z = row // NZ, row % NZ
     width = left[0].shape[1]
@@ -81,7 +83,10 @@
 
     lane = lax.broadcasted_iota(jnp.int32, squares.shape, 1)
 
-    def step(i, acc):
+    def sent_copy(i):
+        return pltpu.make_async_copy(stage.at[i], sent.at[i], sent_sem.at[i])
+
+    def step(to_hbm, i, acc):
         @pl.when(i + 1 < SEQS)
         def _():
             act_copy(i + 1).start()
@@ -95,13 +100,30 @@
         p = lax.dot_general(
             act_buf[i % 2], grads[i], (((0,), (0,)), ((), ())), preferred_element_type=jnp.float32
         )
-        prod[i] = p
+        if to_hbm:
+            stage[i] = p
+            sent_copy(i).start()
+        else:
+            kept[i - SENT] = p
         return jnp.where(lane == seq_of(i), jnp.sum(p * p), acc)
 
-    squares[...] = lax.fori_loop(0, SEQS, step, jnp.zeros(squares.shape, jnp.float32))
-
-
-def combine_kernel(parts, prod, out, norms, out_buf, sem):
+    acc = jnp.zeros(squares.shape, jnp.float32)
+    acc = lax.fori_loop(0, SENT, functools.partial(step, True), acc)
+    squares[...] = lax.fori_loop(SENT, SEQS, functools.partial(step, False), acc)
+    for i in range(SENT):
+        sent_copy(i).wait()
+
+
+def combine_kernel(parts, kept, sent, out, norms, out_buf, back, sem, back_sem):
+    rows = 128
+    chunks = out.shape[0] // rows
+
+    def back_copy(c):
+        at = pl.ds(pl.multiple_of(c * rows, rows), rows)
+        return pltpu.make_async_copy(sent.at[pl.ds(0, SENT), at], back.at[:, at], back_sem.at[c])
+
+    for c in range(chunks):
+        back_copy(c).start()
     row = lax.axis_index("row")
     y = row // NZ
     squares = jnp.sum(parts[...], axis=0, keepdims=True)
@@ -113,8 +135,6 @@
     for i in range(SEQS):
         seq = 2 * ((y + ORDER[i // 2]) % NY) + i % 2
         factors.append(jnp.sum(jnp.where(lane == seq, scale, 0.0)))
-    rows = 128
-    chunks = out.shape[0] // rows
 
     def copy(c):
         at = pl.ds(pl.multiple_of(c * rows, rows), rows)
@@ -122,9 +142,12 @@
 
     def step(c, carry):
         at = pl.ds(pl.multiple_of(c * rows, rows), rows)
-        total = factors[0] * prod[0, at]
-        for i in range(1, SEQS):
-            total = total + factors[i] * prod[i, at]
+        back_copy(c).wait()
+        total = factors[0] * back[0, at]
+        for i in range(1, SENT):
+            total = total + factors[i] * back[i, at]
+        for i in range(SENT, SEQS):
+            total = total + factors[i] * kept[i - SENT, at]
         out_buf[at] = total.astype(jnp.bfloat16)
         copy(c).start()
         return carry
@@ -150,21 +173,24 @@
 
     anywhere = pl.BlockSpec(memory_space=pl.ANY)
     vmem = pl.BlockSpec(memory_space=pltpu.VMEM)
-    prod, squares = pl.pallas_call(
+    kept, sent, squares = pl.pallas_call(
         products_kernel,
         out_shape=(
-            pltpu.VMEM((SEQS, feats, width), jnp.float32),
+            pltpu.VMEM((SEQS - SENT, feats, width), jnp.float32),
+            jax.ShapeDtypeStruct((SEQS, feats, width), jnp.float32),
             jax.ShapeDtypeStruct((devices, SEQS), jnp.float32),
         ),
         in_specs=[anywhere] * 15,
-        out_specs=(vmem, vmem),
+        out_specs=(vmem, anywhere, vmem),
         scratch_shapes=[
             pltpu.VMEM((SEQS, LEN, width), jnp.bfloat16),
             pltpu.VMEM((2, LEN, feats), jnp.bfloat16),
+            pltpu.VMEM((SENT, feats, width), jnp.float32),
             pltpu.SemaphoreType.DMA((NY,)),
             pltpu.SemaphoreType.DMA((2,)),
+            pltpu.SemaphoreType.DMA((SENT,)),
         ],
-        compiler_params=pltpu.CompilerParams(vmem_limit_bytes=26 << 20),
+        compiler_params=pltpu.CompilerParams(vmem_limit_bytes=32 << 20),
         name="sequence_products",
     )(act_full, *left, *right)
     parts = lax.all_to_all(squares, ("row", "col"), 0, 0, tiled=True)
@@ -174,15 +200,17 @@
             jax.ShapeDtypeStruct((feats, width), jnp.bfloat16),
             jax.ShapeDtypeStruct((1, SEQS), jnp.float32),
         ),
-        in_specs=[vmem, vmem],
+        in_specs=[vmem, vmem, anywhere],
         out_specs=(anywhere, vmem),
         scratch_shapes=[
             pltpu.VMEM((feats, width), jnp.bfloat16),
+            pltpu.VMEM((SENT, feats, width), jnp.float32),
+            pltpu.SemaphoreType.DMA((feats // 128,)),
             pltpu.SemaphoreType.DMA((feats // 128,)),
         ],
         compiler_params=pltpu.CompilerParams(vmem_limit_bytes=16 << 20),
         name="scaled_sum",
-    )(parts, prod)
+    )(parts, kept, sent)
     return (weight_grad, norms.reshape(SEQS))
 
 

time: 190 us -> 171 us (0.900)
  local copies, waits for them, and re-layouts: 22.5 us -> 4.38 us
    unnamed x42 -> x32, local copies, waits for them, and re-layouts: 21 us -> 2.87 us
    pallas_call x1, Pallas kernels: 25.6 us -> 21.9 us  [body(): pl.pallas_call(products_kernel, out_shape=(pltpu.VMEM((SEQS - SENT, feats...]
    pallas_call x1, Pallas kernels: 3.33 us -> 6.19 us  [body(): pl.pallas_call(combine_kernel, out_shape=(jax.ShapeDtypeStruct((feats, wi...]
where the time goes in v3:
time: 171 us
  waiting for transfers between devices  58 us (34%)
  starting transfers between devices  36.3 us (21%)
  blocking collectives  28.6 us (17%)
  Pallas kernels  28.1 us (16%)
  between operations  14.5 us (8%)
  local copies, waits for them, and re-layouts  4.38 us (3%)
    ppermute x16, waiting for transfers between devices, z_shift(): return lax.ppermute(value, 'row', pairs)  40.8 us
    all_to_all x1, blocking collectives, body(): parts = lax.all_to_all(squares, ('row', 'col'), 0, 0, tiled=True)  28.6 us
    ppermute x16, starting transfers between devices, z_shift(): return lax.ppermute(value, 'row', pairs)  25.2 us
    pallas_call x1, Pallas kernels, body(): pl.pallas_call(products_kernel, out_shape=(pltpu.VMEM((SEQS - SENT, feats...  21.9 us
    ppermute x8, waiting for transfers between devices, y_shift(): return lax.ppermute(value, 'row', pairs)  16.5 us
    ppermute x8, starting transfers between devices, y_shift(): return lax.ppermute(value, 'row', pairs)  11.1 us
    pallas_call x1, Pallas kernels, body(): pl.pallas_call(combine_kernel, out_shape=(jax.ShapeDtypeStruct((feats, wi...  6.19 us
  transfers between devices with their start and end apart: 25, of which 8 were waited for; matrix products, arithmetic and copies ran while one was open for 1% of the time, Pallas kernels for 0%

profile of v3, /device:TPU:1, one launch (start us, length us, event | category | flops | bytes accessed | tf_op | source)
XLA Modules:
  0.0 170.6 jit_solution(14552231466838767793)
XLA Ops:
  10.0 2.2 %collective-permute-start.13 = (bf16[192,512]{1,0:T(8,128)(2,1)S(1)}, bf16[192,512]{1,0:T(8,128)(2,1)S(1)}, u32[]{:S(2)}, u32[]{:S(2)}) collective-permute-start(bf16[192,512]{1,0:T(8,128)(2,1)S(1)} %get-tuple-element.12), channel_id=1, source_target_pairs={{0,64},{8,72},{16,80},{24,88},{32,96},{40,104},{48,112},{56,120},{... | collective-permute-start | bytes 589832 | tf_op jit(solution)/shard_map/ppermute | solution.py:29
  12.2 1.5 collective-permute-start.12
  13.8 1.6 collective-permute-start.3
  15.4 3.9 %collective-permute-start = (bf16[192,512]{1,0:T(8,128)(2,1)S(1)}, bf16[192,512]{1,0:T(8,128)(2,1)S(1)}, u32[]{:S(2)}, u32[]{:S(2)}) collective-permute-start(bf16[192,512]{1,0:T(8,128)(2,1)S(1)} %get-tuple-element.15), channel_id=1, source_target_pairs={{0,56},{8,0},{16,8},{24,16},{32,24},{40,32},{48,40},{56,48},{64,12... | collective-permute-start | bytes 589832 | tf_op jit(solution)/shard_map/ppermute | solution.py:24
  19.5 2.7 %collective-permute-start.15 = (bf16[96,512]{1,0:T(8,128)(2,1)S(1)}, bf16[96,512]{1,0:T(8,128)(2,1)S(1)}, u32[]{:S(2)}, u32[]{:S(2)}) collective-permute-start(bf16[96,512]{1,0:T(8,128)(2,1)S(1)} %slice.47), channel_id=1, source_target_pairs={{0,192},{8,200},{16,208},{24,216},{32,224},{40,232},{48,240},{56,2... | collective-permute-start | bytes 294920 | tf_op jit(solution)/shard_map/ppermute | solution.py:29
  22.2 1.3 collective-permute-done.3
  23.5 3.1 %collective-permute-start.1 = (bf16[192,512]{1,0:T(8,128)(2,1)S(1)}, bf16[192,512]{1,0:T(8,128)(2,1)S(1)}, u32[]{:S(2)}, u32[]{:S(2)}) collective-permute-start(bf16[192,512]{1,0:T(8,128)(2,1)S(1)} %collective-permute-done), channel_id=1, source_target_pairs={{0,56},{8,0},{16,8},{24,16},{32,24},{40,32},{48,40},{56,48},{64,12... | collective-permute-start | bytes 589832 | tf_op jit(solution)/shard_map/ppermute | solution.py:24
  26.7 2.9 %collective-permute-done.4 = bf16[192,512]{1,0:T(8,128)(2,1)S(1)} collective-permute-done((bf16[192,512]{1,0:T(8,128)(2,1)S(1)}, bf16[192,512]{1,0:T(8,128)(2,1)S(1)}, u32[]{:S(2)}, u32[]{:S(2)}) %collective-permute-start.4) | collective-permute-done | bytes 196640 | tf_op jit(solution)/shard_map/ppermute | solution.py:24
  29.5 2.8 %collective-permute-start.2 = (bf16[192,512]{1,0:T(8,128)(2,1)S(1)}, bf16[192,512]{1,0:T(8,128)(2,1)S(1)}, u32[]{:S(2)}, u32[]{:S(2)}) collective-permute-start(bf16[192,512]{1,0:T(8,128)(2,1)S(1)} %collective-permute-done.1), channel_id=1, source_target_pairs={{0,56},{8,0},{16,8},{24,16},{32,24},{40,32},{48,40},{56,48},{64,12... | collective-permute-start | bytes 589832 | tf_op jit(solution)/shard_map/ppermute | solution.py:24
  32.4 2.7 %collective-permute-start.16 = (bf16[768,512]{1,0:T(8,128)(2,1)S(1)}, bf16[768,512]{1,0:T(8,128)(2,1)S(1)}, u32[]{:S(2)}, u32[]{:S(2)}) collective-permute-start(bf16[768,512]{1,0:T(8,128)(2,1)S(1)} %constant_dynamic-update-slice_fusion.9.refs_6_), channel_id=1, source_target_pairs={{0,56},{8,0},{16,8},{24,16},{32,24},{40,32},{48,40},{56,48},{64,12... | collective-permute-start | bytes 2359304 | tf_op jit(solution)/shard_map/ppermute | solution.py:24
  35.8 2.7 %collective-permute-start.7 = (bf16[96,512]{1,0:T(8,128)(2,1)S(1)}, bf16[96,512]{1,0:T(8,128)(2,1)S(1)}, u32[]{:S(2)}, u32[]{:S(2)}) collective-permute-start(bf16[96,512]{1,0:T(8,128)(2,1)S(1)} %slice.42), channel_id=1, source_target_pairs={{0,56},{8,0},{16,8},{24,16},{32,24},{40,32},{48,40},{56,48},{64,12... | collective-permute-start | bytes 294920 | tf_op jit(solution)/shard_map/ppermute | solution.py:24
  38.6 16.4 %collective-permute-done.6 = bf16[96,512]{1,0:T(8,128)(2,1)S(1)} collective-permute-done((bf16[96,512]{1,0:T(8,128)(2,1)S(1)}, bf16[96,512]{1,0:T(8,128)(2,1)S(1)}, u32[]{:S(2)}, u32[]{:S(2)}) %collective-permute-start.6) | collective-permute-done | bytes 98336 | tf_op jit(solution)/shard_map/ppermute | solution.py:24
  55.1 2.7 %collective-permute-start.8 = (bf16[1536,512]{1,0:T(8,128)(2,1)S(1)}, bf16[1536,512]{1,0:T(8,128)(2,1)S(1)}, u32[]{:S(2)}, u32[]{:S(2)}) collective-permute-start(bf16[1536,512]{1,0:T(8,128)(2,1)S(1)} %constant_dynamic-update-slice_fusion.refs_1_), channel_id=1, source_target_pairs={{0,192},{8,200},{16,208},{24,216},{32,224},{40,232},{48,240},{56,2... | collective-permute-start | bytes 4718600 | tf_op jit(solution)/shard_map/ppermute | solution.py:29
  57.8 2.7 %collective-permute-start.17 = (bf16[768,512]{1,0:T(8,128)(2,1)S(1)}, bf16[768,512]{1,0:T(8,128)(2,1)S(1)}, u32[]{:S(2)}, u32[]{:S(2)}) collective-permute-start(bf16[768,512]{1,0:T(8,128)(2,1)S(1)} %collective-permute-done.16.refs_7_), channel_id=1, source_target_pairs={{0,56},{8,0},{16,8},{24,16},{32,24},{40,32},{48,40},{56,48},{64,12... | collective-permute-start | bytes 2359304 | tf_op jit(solution)/shard_map/ppermute | solution.py:24
  60.5 14.3 %collective-permute-done.20.refs_13_ = bf16[768,512]{1,0:T(8,128)(2,1)S(1)} collective-permute-done((bf16[768,512]{1,0:T(8,128)(2,1)S(1)}, bf16[768,512]{1,0:T(8,128)(2,1)S(1)}, u32[]{:S(2)}, u32[]{:S(2)}) %collective-permute-start.20) | collective-permute-done | bytes 786464 | tf_op jit(solution)/shard_map/ppermute | solution.py:24
  74.8 2.7 %collective-permute-start.18 = (bf16[768,512]{1,0:T(8,128)(2,1)S(1)}, bf16[768,512]{1,0:T(8,128)(2,1)S(1)}, u32[]{:S(2)}, u32[]{:S(2)}) collective-permute-start(bf16[768,512]{1,0:T(8,128)(2,1)S(1)} %collective-permute-done.17.refs_8_), channel_id=1, source_target_pairs={{0,56},{8,0},{16,8},{24,16},{32,24},{40,32},{48,40},{56,48},{64,12... | collective-permute-start | bytes 2359304 | tf_op jit(solution)/shard_map/ppermute | solution.py:24
  77.5 11.9 %collective-permute-done.9.refs_5_ = bf16[1536,512]{1,0:T(8,128)(2,1)S(1)} collective-permute-done((bf16[1536,512]{1,0:T(8,128)(2,1)S(1)}, bf16[1536,512]{1,0:T(8,128)(2,1)S(1)}, u32[]{:S(2)}, u32[]{:S(2)}) %collective-permute-start.9) | collective-permute-done | bytes 1572896 | tf_op jit(solution)/shard_map/ppermute | solution.py:29
  90.6 1.8 %collective-permute-start.11 = (bf16[768,512]{1,0:T(8,128)(2,1)S(1)}, bf16[768,512]{1,0:T(8,128)(2,1)S(1)}, u32[]{:S(2)}, u32[]{:S(2)}) collective-permute-start(bf16[768,512]{1,0:T(8,128)(2,1)S(1)} %slice.44), channel_id=1, source_target_pairs={{0,192},{8,200},{16,208},{24,216},{32,224},{40,232},{48,240},{56,2... | collective-permute-start | bytes 2359304 | tf_op jit(solution)/shard_map/ppermute | solution.py:29
  92.5 2.7 %collective-permute-start.23 = (bf16[384,512]{1,0:T(8,128)(2,1)S(1)}, bf16[384,512]{1,0:T(8,128)(2,1)S(1)}, u32[]{:S(2)}, u32[]{:S(2)}) collective-permute-start(bf16[384,512]{1,0:T(8,128)(2,1)S(1)} %slice.49), channel_id=1, source_target_pairs={{0,56},{8,0},{16,8},{24,16},{32,24},{40,32},{48,40},{56,48},{64,12... | collective-permute-start | bytes 1179656 | tf_op jit(solution)/shard_map/ppermute | solution.py:24
  95.3 5.3 %collective-permute-done.22.refs_10_ = bf16[384,512]{1,0:T(8,128)(2,1)S(1)} collective-permute-done((bf16[384,512]{1,0:T(8,128)(2,1)S(1)}, bf16[384,512]{1,0:T(8,128)(2,1)S(1)}, u32[]{:S(2)}, u32[]{:S(2)}) %collective-permute-start.22) | collective-permute-done | bytes 393248 | tf_op jit(solution)/shard_map/ppermute | solution.py:24
  101.3 4.7 %collective-permute-done.10.refs_3_ = bf16[768,512]{1,0:T(8,128)(2,1)S(1)} collective-permute-done((bf16[768,512]{1,0:T(8,128)(2,1)S(1)}, bf16[768,512]{1,0:T(8,128)(2,1)S(1)}, u32[]{:S(2)}, u32[]{:S(2)}) %collective-permute-start.10) | collective-permute-done | bytes 786464 | tf_op jit(solution)/shard_map/ppermute | solution.py:29
  107.1 21.9 %sequence_products.1 = (f32[5,896,1024]{2,1,0:T(8,128)S(1)}, f32[8,896,1024]{2,1,0:T(8,128)}, f32[256,8]{1,0:T(8,128)S(1)}) custom-call(bf16[6144,896]{1,0:T(8,128)(2,1)} %all-gather.2.cloned.1.call-done.refs_0_, bf16[1536,512]{1,0:T(8,128)(2,1)} %copy-done.4, bf16[1536,512]{1,0:T(8,128)(2,1)} %copy-done.3, ...), custom_call_target="tpu_custom_call" | custom-call | tf_op jit(solution)/shard_map/sequence_products/pallas_call | solution.py:176
  128.9 28.6 %all_to_all.11 = f32[256,1,8]{2,1,0:T(1,128)S(1)} all-to-all(f32[256,1,8]{2,1,0:T(1,128)S(1)} %bitcast.7), channel_id=1, replica_groups=mesh['row'=32,'col'=8] {'row','col'}, dimensions={0} | all-to-all | bytes 16384 | tf_op jit(solution)/shard_map/all_to_all | solution.py:196
  157.5 6.2 %scaled_sum.1 = (bf16[896,1024]{1,0:T(8,128)(2,1)}, f32[1,8]{1,0:T(1,128)}) custom-call(f32[256,8]{1,0:T(8,128)S(1)} %bitcast.6, f32[5,896,1024]{2,1,0:T(8,128)S(1)} %get-tuple-element.8.kept, f32[8,896,1024]{2,1,0:T(8,128)} %get-tuple-element.9.sent), custom_call_target="tpu_custom_call" | custom-call | tf_op jit(solution)/shard_map/scaled_sum/pallas_call | solution.py:197
  (76 shorter events, 7.0 us)
Async XLA Ops:
  7.2 98.9 %all-gather.2.cloned.1.call-start = ((), (), s32[]{:S(2)}) async-start(), calls=%async_computation.1 | async-start | bytes 12386304 | tf_op jit(solution)/shard_map/all_gather | solution.py:164
  10.0 9.3 %collective-permute-start.13 = (bf16[192,512]{1,0:T(8,128)(2,1)S(1)}, bf16[192,512]{1,0:T(8,128)(2,1)S(1)}, u32[]{:S(2)}, u32[]{:S(2)}) collective-permute-start(bf16[192,512]{1,0:T(8,128)(2,1)S(1)} %get-tuple-element.12), channel_id=1, source_target_pairs={{0,64},{8,72},{16,80},{24,88},{32,96},{40,104},{48,112},{56,120},{... | collective-permute-start | bytes 589832 | tf_op jit(solution)/shard_map/ppermute | solution.py:29
  12.2 7.2 %collective-permute-start.12 = (bf16[192,512]{1,0:T(8,128)(2,1)S(1)}, bf16[192,512]{1,0:T(8,128)(2,1)S(1)}, u32[]{:S(2)}, u32[]{:S(2)}) collective-permute-start(bf16[192,512]{1,0:T(8,128)(2,1)S(1)} %get-tuple-element.12), channel_id=1, source_target_pairs={{0,192},{8,200},{16,208},{24,216},{32,224},{40,232},{48,240},{56,2... | collective-permute-start | bytes 589832 | tf_op jit(solution)/shard_map/ppermute | solution.py:29
  13.8 9.7 %collective-permute-start.3 = (bf16[192,512]{1,0:T(8,128)(2,1)S(1)}, bf16[192,512]{1,0:T(8,128)(2,1)S(1)}, u32[]{:S(2)}, u32[]{:S(2)}) collective-permute-start(bf16[192,512]{1,0:T(8,128)(2,1)S(1)} %get-tuple-element.15), channel_id=1, source_target_pairs={{0,8},{8,16},{16,24},{24,32},{32,40},{40,48},{48,56},{56,0},{64,72... | collective-permute-start | bytes 589832 | tf_op jit(solution)/shard_map/ppermute | solution.py:24
  15.4 8.1 %collective-permute-start = (bf16[192,512]{1,0:T(8,128)(2,1)S(1)}, bf16[192,512]{1,0:T(8,128)(2,1)S(1)}, u32[]{:S(2)}, u32[]{:S(2)}) collective-permute-start(bf16[192,512]{1,0:T(8,128)(2,1)S(1)} %get-tuple-element.15), channel_id=1, source_target_pairs={{0,56},{8,0},{16,8},{24,16},{32,24},{40,32},{48,40},{56,48},{64,12... | collective-permute-start | bytes 589832 | tf_op jit(solution)/shard_map/ppermute | solution.py:24
  19.3 7.3 %collective-permute-start.14 = (bf16[96,512]{1,0:T(8,128)(2,1)S(1)}, bf16[96,512]{1,0:T(8,128)(2,1)S(1)}, u32[]{:S(2)}, u32[]{:S(2)}) collective-permute-start(bf16[96,512]{1,0:T(8,128)(2,1)S(1)} %slice.46), channel_id=1, source_target_pairs={{0,64},{8,72},{16,80},{24,88},{32,96},{40,104},{48,112},{56,120},{... | collective-permute-start | bytes 294920 | tf_op jit(solution)/shard_map/ppermute | solution.py:29
  19.5 7.2 %collective-permute-start.15 = (bf16[96,512]{1,0:T(8,128)(2,1)S(1)}, bf16[96,512]{1,0:T(8,128)(2,1)S(1)}, u32[]{:S(2)}, u32[]{:S(2)}) collective-permute-start(bf16[96,512]{1,0:T(8,128)(2,1)S(1)} %slice.47), channel_id=1, source_target_pairs={{0,192},{8,200},{16,208},{24,216},{32,224},{40,232},{48,240},{56,2... | collective-permute-start | bytes 294920 | tf_op jit(solution)/shard_map/ppermute | solution.py:29
  23.5 6.1 %collective-permute-start.4 = (bf16[192,512]{1,0:T(8,128)(2,1)S(1)}, bf16[192,512]{1,0:T(8,128)(2,1)S(1)}, u32[]{:S(2)}, u32[]{:S(2)}) collective-permute-start(bf16[192,512]{1,0:T(8,128)(2,1)S(1)} %collective-permute-done.3), channel_id=1, source_target_pairs={{0,8},{8,16},{16,24},{24,32},{32,40},{40,48},{48,56},{56,0},{64,72... | collective-permute-start | bytes 589832 | tf_op jit(solution)/shard_map/ppermute | solution.py:24
  29.5 6.1 %collective-permute-start.5 = (bf16[192,512]{1,0:T(8,128)(2,1)S(1)}, bf16[192,512]{1,0:T(8,128)(2,1)S(1)}, u32[]{:S(2)}, u32[]{:S(2)}) collective-permute-start(bf16[192,512]{1,0:T(8,128)(2,1)S(1)} %collective-permute-done.4), channel_id=1, source_target_pairs={{0,8},{8,16},{16,24},{24,32},{32,40},{40,48},{48,56},{56,0},{64,72... | collective-permute-start | bytes 589832 | tf_op jit(solution)/shard_map/ppermute | solution.py:24
  29.5 6.2 %collective-permute-start.2 = (bf16[192,512]{1,0:T(8,128)(2,1)S(1)}, bf16[192,512]{1,0:T(8,128)(2,1)S(1)}, u32[]{:S(2)}, u32[]{:S(2)}) collective-permute-start(bf16[192,512]{1,0:T(8,128)(2,1)S(1)} %collective-permute-done.1), channel_id=1, source_target_pairs={{0,56},{8,0},{16,8},{24,16},{32,24},{40,32},{48,40},{56,48},{64,12... | collective-permute-start | bytes 589832 | tf_op jit(solution)/shard_map/ppermute | solution.py:24
  32.3 25.5 %collective-permute-start.19 = (bf16[768,512]{1,0:T(8,128)(2,1)S(1)}, bf16[768,512]{1,0:T(8,128)(2,1)S(1)}, u32[]{:S(2)}, u32[]{:S(2)}) collective-permute-start(bf16[768,512]{1,0:T(8,128)(2,1)S(1)} %constant_dynamic-update-slice_fusion.9.refs_6_), channel_id=1, source_target_pairs={{0,8},{8,16},{16,24},{24,32},{32,40},{40,48},{48,56},{56,0},{64,72... | collective-permute-start | bytes 2359304 | tf_op jit(solution)/shard_map/ppermute | solution.py:24
  32.4 25.4 %collective-permute-start.16 = (bf16[768,512]{1,0:T(8,128)(2,1)S(1)}, bf16[768,512]{1,0:T(8,128)(2,1)S(1)}, u32[]{:S(2)}, u32[]{:S(2)}) collective-permute-start(bf16[768,512]{1,0:T(8,128)(2,1)S(1)} %constant_dynamic-update-slice_fusion.9.refs_6_), channel_id=1, source_target_pairs={{0,56},{8,0},{16,8},{24,16},{32,24},{40,32},{48,40},{56,48},{64,12... | collective-permute-start | bytes 2359304 | tf_op jit(solution)/shard_map/ppermute | solution.py:24
  35.7 19.3 %collective-permute-start.6 = (bf16[96,512]{1,0:T(8,128)(2,1)S(1)}, bf16[96,512]{1,0:T(8,128)(2,1)S(1)}, u32[]{:S(2)}, u32[]{:S(2)}) collective-permute-start(bf16[96,512]{1,0:T(8,128)(2,1)S(1)} %slice.41), channel_id=1, source_target_pairs={{0,8},{8,16},{16,24},{24,32},{32,40},{40,48},{48,56},{56,0},{64,72... | collective-permute-start | bytes 294920 | tf_op jit(solution)/shard_map/ppermute | solution.py:24
  35.8 19.1 %collective-permute-start.7 = (bf16[96,512]{1,0:T(8,128)(2,1)S(1)}, bf16[96,512]{1,0:T(8,128)(2,1)S(1)}, u32[]{:S(2)}, u32[]{:S(2)}) collective-permute-start(bf16[96,512]{1,0:T(8,128)(2,1)S(1)} %slice.42), channel_id=1, source_target_pairs={{0,56},{8,0},{16,8},{24,16},{32,24},{40,32},{48,40},{56,48},{64,12... | collective-permute-start | bytes 294920 | tf_op jit(solution)/shard_map/ppermute | solution.py:24
  55.0 34.3 %collective-permute-start.9 = (bf16[1536,512]{1,0:T(8,128)(2,1)S(1)}, bf16[1536,512]{1,0:T(8,128)(2,1)S(1)}, u32[]{:S(2)}, u32[]{:S(2)}) collective-permute-start(bf16[1536,512]{1,0:T(8,128)(2,1)S(1)} %constant_dynamic-update-slice_fusion.refs_1_), channel_id=1, source_target_pairs={{0,64},{8,72},{16,80},{24,88},{32,96},{40,104},{48,112},{56,120},{... | collective-permute-start | bytes 4718600 | tf_op jit(solution)/shard_map/ppermute | solution.py:29
  55.1 34.4 %collective-permute-start.8 = (bf16[1536,512]{1,0:T(8,128)(2,1)S(1)}, bf16[1536,512]{1,0:T(8,128)(2,1)S(1)}, u32[]{:S(2)}, u32[]{:S(2)}) collective-permute-start(bf16[1536,512]{1,0:T(8,128)(2,1)S(1)} %constant_dynamic-update-slice_fusion.refs_1_), channel_id=1, source_target_pairs={{0,192},{8,200},{16,208},{24,216},{32,224},{40,232},{48,240},{56,2... | collective-permute-start | bytes 4718600 | tf_op jit(solution)/shard_map/ppermute | solution.py:29
  57.8 16.9 %collective-permute-start.20 = (bf16[768,512]{1,0:T(8,128)(2,1)S(1)}, bf16[768,512]{1,0:T(8,128)(2,1)S(1)}, u32[]{:S(2)}, u32[]{:S(2)}) collective-permute-start(bf16[768,512]{1,0:T(8,128)(2,1)S(1)} %collective-permute-done.19.refs_14_), channel_id=1, source_target_pairs={{0,8},{8,16},{16,24},{24,32},{32,40},{40,48},{48,56},{56,0},{64,72... | collective-permute-start | bytes 2359304 | tf_op jit(solution)/shard_map/ppermute | solution.py:24
  57.8 16.9 %collective-permute-start.17 = (bf16[768,512]{1,0:T(8,128)(2,1)S(1)}, bf16[768,512]{1,0:T(8,128)(2,1)S(1)}, u32[]{:S(2)}, u32[]{:S(2)}) collective-permute-start(bf16[768,512]{1,0:T(8,128)(2,1)S(1)} %collective-permute-done.16.refs_7_), channel_id=1, source_target_pairs={{0,56},{8,0},{16,8},{24,16},{32,24},{40,32},{48,40},{56,48},{64,12... | collective-permute-start | bytes 2359304 | tf_op jit(solution)/shard_map/ppermute | solution.py:24
  74.8 17.6 %collective-permute-start.21 = (bf16[768,512]{1,0:T(8,128)(2,1)S(1)}, bf16[768,512]{1,0:T(8,128)(2,1)S(1)}, u32[]{:S(2)}, u32[]{:S(2)}) collective-permute-start(bf16[768,512]{1,0:T(8,128)(2,1)S(1)} %collective-permute-done.20.refs_13_), channel_id=1, source_target_pairs={{0,8},{8,16},{16,24},{24,32},{32,40},{40,48},{48,56},{56,0},{64,72... | collective-permute-start | bytes 2359304 | tf_op jit(solution)/shard_map/ppermute | solution.py:24
  74.8 17.7 %collective-permute-start.18 = (bf16[768,512]{1,0:T(8,128)(2,1)S(1)}, bf16[768,512]{1,0:T(8,128)(2,1)S(1)}, u32[]{:S(2)}, u32[]{:S(2)}) collective-permute-start(bf16[768,512]{1,0:T(8,128)(2,1)S(1)} %collective-permute-done.17.refs_8_), channel_id=1, source_target_pairs={{0,56},{8,0},{16,8},{24,16},{32,24},{40,32},{48,40},{56,48},{64,12... | collective-permute-start | bytes 2359304 | tf_op jit(solution)/shard_map/ppermute | solution.py:24
  89.4 16.6 %collective-permute-start.10 = (bf16[768,512]{1,0:T(8,128)(2,1)S(1)}, bf16[768,512]{1,0:T(8,128)(2,1)S(1)}, u32[]{:S(2)}, u32[]{:S(2)}) collective-permute-start(bf16[768,512]{1,0:T(8,128)(2,1)S(1)} %slice.43), channel_id=1, source_target_pairs={{0,64},{8,72},{16,80},{24,88},{32,96},{40,104},{48,112},{56,120},{... | collective-permute-start | bytes 2359304 | tf_op jit(solution)/shard_map/ppermute | solution.py:29
  90.6 15.4 %collective-permute-start.11 = (bf16[768,512]{1,0:T(8,128)(2,1)S(1)}, bf16[768,512]{1,0:T(8,128)(2,1)S(1)}, u32[]{:S(2)}, u32[]{:S(2)}) collective-permute-start(bf16[768,512]{1,0:T(8,128)(2,1)S(1)} %slice.44), channel_id=1, source_target_pairs={{0,192},{8,200},{16,208},{24,216},{32,224},{40,232},{48,240},{56,2... | collective-permute-start | bytes 2359304 | tf_op jit(solution)/shard_map/ppermute | solution.py:29
  92.4 8.2 %collective-permute-start.22 = (bf16[384,512]{1,0:T(8,128)(2,1)S(1)}, bf16[384,512]{1,0:T(8,128)(2,1)S(1)}, u32[]{:S(2)}, u32[]{:S(2)}) collective-permute-start(bf16[384,512]{1,0:T(8,128)(2,1)S(1)} %slice.48), channel_id=1, source_target_pairs={{0,8},{8,16},{16,24},{24,32},{32,40},{40,48},{48,56},{56,0},{64,72... | collective-permute-start | bytes 1179656 | tf_op jit(solution)/shard_map/ppermute | solution.py:24
  92.5 8.1 %collective-permute-start.23 = (bf16[384,512]{1,0:T(8,128)(2,1)S(1)}, bf16[384,512]{1,0:T(8,128)(2,1)S(1)}, u32[]{:S(2)}, u32[]{:S(2)}) collective-permute-start(bf16[384,512]{1,0:T(8,128)(2,1)S(1)} %slice.49), channel_id=1, source_target_pairs={{0,56},{8,0},{16,8},{24,16},{32,24},{40,32},{48,40},{56,48},{64,12... | collective-permute-start | bytes 1179656 | tf_op jit(solution)/shard_map/ppermute | solution.py:24
  (12 other events, 172.3 us)
Sparse Core Ops, SparseCore 0:
  9.8 67.4 all-gather.1
